TPU v7x, 512 devices: a whole 4x8x8 slice. The times are simulated.
512 devices in a mesh: dp: 4 (over x), expert: 128 (over z, y, core).
Axes of the slice: x: 4, y: 8, z: 8, core: 2. Of those that a mesh axis runs over, the one named last changes fastest.
Arguments:
- x_rows: bfloat16 [65536, 1024], P(('dp', 'expert')), may hold values from -6 to 6
- expert_ids: int32 [65536, 1], P(('dp', 'expert')), may hold values from 0 to 127; in each aligned block of 128 rows (0 to 127, 128 to 255, ...) at most 2 rows name the same one
- gates: float32 [65536, 1], P(('dp', 'expert')), may hold values from 0.1 to 1
- cotangent: bfloat16 [65536, 1024], P(('dp', 'expert')), may hold values from -6 to 6
- w_gate: bfloat16 [128, 1024, 384], P('expert', 'dp'), may hold values from -0.1875 to 0.1875
- w_up: bfloat16 [128, 1024, 384], P('expert', 'dp'), may hold values from -0.1875 to 0.1875
- w_down: bfloat16 [128, 384, 1024], P('expert', None, 'dp'), may hold values from -0.3125 to 0.3125
Outputs:
- gated_out: bfloat16 [65536, 1024], P(('dp', 'expert'))
- input_grad: bfloat16 [65536, 1024], P(('dp', 'expert'))
- gate_grad: float32 [65536, 1], P(('dp', 'expert'))
- grad_gate: bfloat16 [128, 1024, 384], P('expert', 'dp')
- grad_up: bfloat16 [128, 1024, 384], P('expert', 'dp')
- grad_down: bfloat16 [128, 384, 1024], P('expert', None, 'dp')
Inputs may be any that keep to these rules, and one draw needn't show every extreme that they name: `expert_ids`: among the rows of one device each expert id occurs at most 2 times, and in some device's rows some expert occurs exactly 2 times.
All inputs are finite; a program needn't handle non-finite values.
Results may differ from a plain program's by a relative error of at most 0.009.
Values may be sent and summed in bfloat16 or wider, within the bound.
No kernel may reach another device: no remote copies, remote signals or barrier semaphores. Data moves between devices by JAX's collectives and lax.ppermute only.
A program may use at most 64 MiB of HBM per device.

v0:
```python
import jax
import jax.numpy as jnp
from jax import lax
from jax.sharding import PartitionSpec as P


def expert_rows(rows_in, rows_scaled, proj_gate, proj_up, proj_down):
    gate_act = jnp.dot(rows_in, proj_gate, preferred_element_type=jnp.float32)
    up_act = jnp.dot(rows_in, proj_up, preferred_element_type=jnp.float32)
    sigma = jax.nn.sigmoid(gate_act)
    hidden = (gate_act * sigma * up_act).astype(jnp.bfloat16)
    result = jnp.dot(hidden, proj_down, preferred_element_type=jnp.float32).astype(jnp.bfloat16)
    backed = jnp.dot(rows_scaled, proj_down.T, preferred_element_type=jnp.float32)
    d_gate_act = (backed * up_act * sigma * (1.0 + gate_act * (1.0 - sigma))).astype(jnp.bfloat16)
    d_up_act = (backed * gate_act * sigma).astype(jnp.bfloat16)
    d_input = (
        jnp.dot(d_gate_act, proj_gate.T, preferred_element_type=jnp.float32)
        + jnp.dot(d_up_act, proj_up.T, preferred_element_type=jnp.float32)
    ).astype(jnp.bfloat16)
    grad_g = jnp.dot(rows_in.T, d_gate_act, preferred_element_type=jnp.float32)
    grad_u = jnp.dot(rows_in.T, d_up_act, preferred_element_type=jnp.float32)
    grad_d = jnp.dot(hidden.T, rows_scaled, preferred_element_type=jnp.float32)
    return (result, d_input, (grad_g, grad_u, grad_d), (hidden, d_gate_act, d_up_act))


def per_device(x_rows, expert_ids, gates, cotangent, w_gate, w_up, w_down):
    full_gate, full_up, full_down = (
        lax.all_gather(w_gate, "dp", axis=1, tiled=True),
        lax.all_gather(w_up, "dp", axis=1, tiled=True),
        lax.all_gather(w_down, "dp", axis=2, tiled=True),
    )
    proj_gate = full_gate[0]
    proj_up = full_up[0]
    proj_down = full_down[0]
    experts = lax.axis_size("expert")
    row_count = x_rows.shape[0]
    width = x_rows.shape[1]
    capacity = 2 * row_count // experts
    row_ids = expert_ids[:, 0]
    onehot = (row_ids[:, None] == jnp.arange(experts, dtype=jnp.int32)[None, :]).astype(jnp.int32)
    ranking = jnp.sum((jnp.cumsum(onehot, 0) - onehot) * onehot, 1)
    slot = row_ids * capacity + ranking
    counts = jnp.sum(onehot, 0)
    scaled = (gates * cotangent.astype(jnp.float32)).astype(jnp.bfloat16)
    send_in = (
        jnp.zeros((experts * capacity, width), jnp.bfloat16)
        .at[slot]
        .set(x_rows)
        .reshape(experts, capacity, width)
    )
    send_scaled = (
        jnp.zeros((experts * capacity, width), jnp.bfloat16)
        .at[slot]
        .set(scaled)
        .reshape(experts, capacity, width)
    )
    recv_in, recv_scaled, recv_counts = (
        lax.all_to_all(send_in, "expert", split_axis=0, concat_axis=0, tiled=True),
        lax.all_to_all(send_scaled, "expert", split_axis=0, concat_axis=0, tiled=True),
        lax.all_to_all(
            counts.reshape(experts, 1), "expert", split_axis=0, concat_axis=0, tiled=True
        ),
    )
    flat_in = recv_in.reshape(experts * capacity, width)
    flat_scaled = recv_scaled.reshape(experts * capacity, width)
    slot_out, slot_grad, grads, acts = expert_rows(
        flat_in, flat_scaled, proj_gate, proj_up, proj_down
    )
    back_result, back_input = (
        lax.all_to_all(
            slot_out.reshape(experts, capacity, width),
            "expert",
            split_axis=0,
            concat_axis=0,
            tiled=True,
        ),
        lax.all_to_all(
            slot_grad.reshape(experts, capacity, width),
            "expert",
            split_axis=0,
            concat_axis=0,
            tiled=True,
        ),
    )
    row_out = back_result.reshape(experts * capacity, width)[slot]
    input_grad = back_input.reshape(experts * capacity, width)[slot]
    gated_out = (gates * row_out.astype(jnp.float32)).astype(jnp.bfloat16)
    gate_grad = jnp.sum(
        cotangent.astype(jnp.float32) * row_out.astype(jnp.float32), 1, keepdims=True
    )
    summed_gate, summed_up, summed_down = (
        lax.psum_scatter(
            grads[0][None].astype(jnp.bfloat16), "dp", scatter_dimension=1, tiled=True
        ).astype(jnp.float32),
        lax.psum_scatter(
            grads[1][None].astype(jnp.bfloat16), "dp", scatter_dimension=1, tiled=True
        ).astype(jnp.float32),
        lax.psum_scatter(
            grads[2][None].astype(jnp.bfloat16), "dp", scatter_dimension=2, tiled=True
        ).astype(jnp.float32),
    )
    return (
        gated_out,
        input_grad,
        gate_grad,
        summed_gate.astype(jnp.bfloat16),
        summed_up.astype(jnp.bfloat16),
        summed_down.astype(jnp.bfloat16),
    )


def solution(mesh):
    in_specs = (
        P(("dp", "expert"), None),
        P(("dp", "expert"), None),
        P(("dp", "expert"), None),
        P(("dp", "expert"), None),
        P("expert", "dp", None),
        P("expert", "dp", None),
        P("expert", None, "dp"),
    )
    out_specs = (
        P(("dp", "expert"), None),
        P(("dp", "expert"), None),
        P(("dp", "expert"), None),
        P("expert", "dp", None),
        P("expert", "dp", None),
        P("expert", None, "dp"),
    )
    return jax.shard_map(
        per_device, mesh=mesh, in_specs=in_specs, out_specs=out_specs, check_vma=False
    )
```

profile of v0, /device:TPU:8, one launch (start us, length us, event | category | flops | bytes accessed | tf_op | source)
XLA Modules:
  0.0 194.1 jit_solution(5530824760676524770)
XLA Ops:
  7.2 0.7 fusion.23
  8.1 0.8 select_reduce_fusion
  8.9 0.7 fusion.24
  9.6 1.7 scatter_custom_fusion
  11.3 1.0 reshape.40
  12.3 17.4 %all-to-all-start = ((bf16[128,2,1024]{2,1,0:T(2,128)(2,1)}), bf16[128,2,1024]{2,1,0:T(2,128)(2,1)S(1)}, u32[]{:S(2)}, u32[]{:S(2)}) async-start(bf16[128,2,1024]{2,1,0:T(2,128)(2,1)} %reshape.40), calls=%async_computation | async-start | bytes 1048576 | tf_op jit(solution)/shard_map/all_to_all | solution.py:58
  29.7 1.4 scatter_custom_fusion.1
  31.1 1.0 reshape.44
  32.1 14.0 %all_gather.9 = bf16[1,1024,384]{2,1,0:T(8,128)(2,1)S(1)} all-gather(bf16[1,256,384]{2,1,0:T(8,128)(2,1)S(1)} %copy-done.6), channel_id=1, replica_groups=mesh['dp'=4,'expert'=128] {'dp'}, dimensions={1}, use_global_device_ids=true | all-gather | bytes 983040 | tf_op jit(solution)/shard_map/all_gather | solution.py:28
  46.1 3.8 %all-to-all-done = bf16[128,2,1024]{2,1,0:T(2,128)(2,1)S(1)} async-done(((bf16[128,2,1024]{2,1,0:T(2,128)(2,1)}), bf16[128,2,1024]{2,1,0:T(2,128)(2,1)S(1)}, u32[]{:S(2)}, u32[]{:S(2)}) %all-to-all-start) | async-done | bytes 524320 | tf_op jit(solution)/shard_map/all_to_all | solution.py:58
  49.9 10.5 %all-to-all-start.2 = ((bf16[128,2,1024]{2,1,0:T(2,128)(2,1)}), bf16[128,2,1024]{2,1,0:T(2,128)(2,1)}, u32[]{:S(2)}, u32[]{:S(2)}) async-start(bf16[128,2,1024]{2,1,0:T(2,128)(2,1)} %reshape.44), calls=%async_computation.2 | async-start | bytes 1048576 | tf_op jit(solution)/shard_map/all_to_all | solution.py:59
  60.5 13.7 %all_gather.10 = bf16[1,1024,384]{2,1,0:T(8,128)(2,1)S(1)} all-gather(bf16[1,256,384]{2,1,0:T(8,128)(2,1)S(1)} %copy-done.7), channel_id=1, replica_groups=mesh['dp'=4,'expert'=128] {'dp'}, dimensions={1}, use_global_device_ids=true | all-gather | bytes 983040 | tf_op jit(solution)/shard_map/all_gather | solution.py:29
  74.2 14.3 %all_gather.11 = bf16[1,384,1024]{2,1,0:T(8,128)(2,1)S(1)} all-gather(bf16[1,384,256]{2,1,0:T(8,128)(2,1)S(1)} %copy-done.8), channel_id=1, replica_groups=mesh['dp'=4,'expert'=128] {'dp'}, dimensions={2}, use_global_device_ids=true | all-gather | bytes 983040 | tf_op jit(solution)/shard_map/all_gather | solution.py:30
  88.7 1.2 fusion.12
  89.9 1.2 fusion.8
  91.1 1.2 reshape.45
  92.3 2.4 %multiply_convert_fusion = (bf16[256,384]{1,0:T(8,128)(2,1)}, bf16[256,384]{1,0:T(8,128)(2,1)S(1)}, bf16[256,384]{1,0:T(8,128)(2,1)}) fusion(f32[256,384]{1,0:T(8,128)} %fusion.12, f32[256,384]{1,0:T(8,128)} %fusion.8, bf16[256,1024]{1,0:T(8,128)(2,1)S(1)} %reshape.45, bf16[1,384,1024]{2,1,0:T(8,128)(2,1)S(1)} %all_gather.11), kind=kOutput, calls=%fused_computation.29 | convolution fusion | flops 202899456 | bytes 2686976 | tf_op jit(solution)/shard_map/dot_general | solution.py:13
  94.7 0.7 copy-done.4
  95.4 1.3 fusion
  96.8 2.3 %fusion.1 = bf16[1,1024,384]{2,1,0:T(8,128)(2,1)} fusion(bf16[256,1024]{1,0:T(8,128)(2,1)S(1)} %reshape.41, bf16[256,384]{1,0:T(8,128)(2,1)} %get-tuple-element.6), kind=kOutput, calls=%fused_computation.10 | convolution fusion | flops 201719808 | bytes 1507328 | tf_op jit(solution)/shard_map/dot_general | solution.py:21
  99.1 1.4 convolution_convert_fusion.3
  100.5 1.0 reshape.42
  101.5 13.8 %all-to-all-start.1 = ((bf16[128,2,1024]{2,1,0:T(2,128)(2,1)}), bf16[128,2,1024]{2,1,0:T(2,128)(2,1)S(1)}, u32[]{:S(2)}, u32[]{:S(2)}) async-start(bf16[128,2,1024]{2,1,0:T(2,128)(2,1)} %reshape.42), calls=%async_computation.1 | async-start | bytes 1048576 | tf_op jit(solution)/shard_map/all_to_all | solution.py:70
  115.5 1.3 fusion.2
  118.2 1.0 reshape.46
  119.2 16.2 %all-to-all-done.1 = bf16[128,2,1024]{2,1,0:T(2,128)(2,1)S(1)} async-done(((bf16[128,2,1024]{2,1,0:T(2,128)(2,1)}), bf16[128,2,1024]{2,1,0:T(2,128)(2,1)S(1)}, u32[]{:S(2)}, u32[]{:S(2)}) %all-to-all-start.1) | async-done | bytes 524320 | tf_op jit(solution)/shard_map/all_to_all | solution.py:70
  135.4 5.8 %all-to-all-start.3 = ((bf16[128,2,1024]{2,1,0:T(2,128)(2,1)}), bf16[128,2,1024]{2,1,0:T(2,128)(2,1)S(1)}, u32[]{:S(2)}, u32[]{:S(2)}) async-start(bf16[128,2,1024]{2,1,0:T(2,128)(2,1)} %reshape.46), calls=%async_computation.3 | async-start | bytes 1048576 | tf_op jit(solution)/shard_map/all_to_all | solution.py:77
  141.4 0.9 gather_fusion
  142.3 19.1 %all-to-all-done.3 = bf16[128,2,1024]{2,1,0:T(2,128)(2,1)S(1)} async-done(((bf16[128,2,1024]{2,1,0:T(2,128)(2,1)}), bf16[128,2,1024]{2,1,0:T(2,128)(2,1)S(1)}, u32[]{:S(2)}, u32[]{:S(2)}) %all-to-all-start.3) | async-done | bytes 524320 | tf_op jit(solution)/shard_map/all_to_all | solution.py:77
  161.6 1.6 gather_fusion.1
  163.2 1.3 fusion.16
  164.5 23.1 %reduce-scatter.8.cloned.1.call-done = bf16[1,384,256]{2,1,0:T(8,128)(2,1)} async-done(((bf16[1,384,1024]{2,1,0:T(8,128)(2,1)}), bf16[1,384,256]{2,1,0:T(8,128)(2,1)}) %reduce-scatter.8.cloned.1.call-update) | async-done | bytes 196624 | tf_op jit(solution)/shard_map/reduce_scatter | solution.py:98
  (35 shorter events, 2.6 us)
Async XLA Ops:
  11.3 18.4 %copy-start = (bf16[128,1024]{1,0:T(8,128)(2,1)S(1)}, bf16[128,1024]{1,0:T(8,128)(2,1)}, u32[]{:S(2)}) copy-start(bf16[128,1024]{1,0:T(8,128)(2,1)} %param.10) | copy-start | bytes 786436
  11.3 18.4 %copy-start.9 = (f32[128,1]{0,1:T(1,128)S(1)}, f32[128,1]{0,1:T(1,128)}, u32[]{:S(2)}) copy-start(f32[128,1]{0,1:T(1,128)} %param.9) | copy-start | bytes 1540
  12.3 37.6 %all-to-all-start = ((bf16[128,2,1024]{2,1,0:T(2,128)(2,1)}), bf16[128,2,1024]{2,1,0:T(2,128)(2,1)S(1)}, u32[]{:S(2)}, u32[]{:S(2)}) async-start(bf16[128,2,1024]{2,1,0:T(2,128)(2,1)} %reshape.40), calls=%async_computation | async-start | bytes 1048576 | tf_op jit(solution)/shard_map/all_to_all | solution.py:58
  29.7 2.4 %copy-start.6 = (bf16[1,256,384]{2,1,0:T(8,128)(2,1)S(1)}, bf16[1,256,384]{2,1,0:T(8,128)(2,1)}, u32[]{:S(2)}) copy-start(bf16[1,256,384]{2,1,0:T(8,128)(2,1)} %param.11) | copy-start | bytes 589828
  32.1 28.4 %copy-start.7 = (bf16[1,256,384]{2,1,0:T(8,128)(2,1)S(1)}, bf16[1,256,384]{2,1,0:T(8,128)(2,1)}, u32[]{:S(2)}) copy-start(bf16[1,256,384]{2,1,0:T(8,128)(2,1)} %param.12) | copy-start | bytes 589828
  46.1 28.1 %copy-start.8 = (bf16[1,384,256]{2,1,0:T(8,128)(2,1)S(1)}, bf16[1,384,256]{2,1,0:T(8,128)(2,1)}, u32[]{:S(2)}) copy-start(bf16[1,384,256]{2,1,0:T(8,128)(2,1)} %param.13) | copy-start | bytes 589828
  49.9 41.2 %all-to-all-start.2 = ((bf16[128,2,1024]{2,1,0:T(2,128)(2,1)}), bf16[128,2,1024]{2,1,0:T(2,128)(2,1)}, u32[]{:S(2)}, u32[]{:S(2)}) async-start(bf16[128,2,1024]{2,1,0:T(2,128)(2,1)} %reshape.44), calls=%async_computation.2 | async-start | bytes 1048576 | tf_op jit(solution)/shard_map/all_to_all | solution.py:59
  60.4 104.1 %reduce-scatter.4.cloned.1.call-start = ((), (), s32[]{:S(2)}) async-start(), calls=%async_computation.7 | async-start | bytes 983040 | tf_op jit(solution)/shard_map/reduce_scatter | solution.py:92
  94.7 0.7 copy-start.4
  96.7 67.8 %reduce-scatter.6.cloned.1.call-start = ((), (), s32[]{:S(2)}) async-start(), calls=%async_computation.8 | async-start | bytes 983040 | tf_op jit(solution)/shard_map/reduce_scatter | solution.py:95
  100.5 15.0 %copy-start.3 = (bf16[256,384]{1,0:T(8,128)(2,1)S(1)}, bf16[256,384]{1,0:T(8,128)(2,1)}, u32[]{:S(2)}) copy-start(bf16[256,384]{1,0:T(8,128)(2,1)} %get-tuple-element.8) | copy-start | bytes 589828
  101.5 34.0 %all-to-all-start.1 = ((bf16[128,2,1024]{2,1,0:T(2,128)(2,1)}), bf16[128,2,1024]{2,1,0:T(2,128)(2,1)S(1)}, u32[]{:S(2)}, u32[]{:S(2)}) async-start(bf16[128,2,1024]{2,1,0:T(2,128)(2,1)} %reshape.42), calls=%async_computation.1 | async-start | bytes 1048576 | tf_op jit(solution)/shard_map/all_to_all | solution.py:70
  115.3 1.6 copy-start.5
  115.3 72.3 %reduce-scatter.8.cloned.1.call-start = ((), (), s32[]{:S(2)}) async-start(), calls=%async_computation.9 | async-start | bytes 983040 | tf_op jit(solution)/shard_map/reduce_scatter | solution.py:98
  116.8 0.9 copy-start.2
  135.4 26.0 %all-to-all-start.3 = ((bf16[128,2,1024]{2,1,0:T(2,128)(2,1)}), bf16[128,2,1024]{2,1,0:T(2,128)(2,1)S(1)}, u32[]{:S(2)}, u32[]{:S(2)}) async-start(bf16[128,2,1024]{2,1,0:T(2,128)(2,1)} %reshape.46), calls=%async_computation.3 | async-start | bytes 1048576 | tf_op jit(solution)/shard_map/all_to_all | solution.py:77
  161.6 1.6 copy-start.1
Sparse Core Ops, SparseCore 0:
  96.9 28.3 reduce-scatter.3
  128.7 27.6 reduce-scatter.5
  159.8 27.7 reduce-scatter.7
where the time goes:
time: 195 us; the launch traced here: 194 us
  waiting for transfers between devices  62.2 us (32%)
  starting transfers between devices  47.7 us (24%)
  blocking collectives  42 us (22%)
  between operations  14 us (7%)
  matrix products  12 us (6%)
  local copies, waits for them, and re-layouts  11.1 us (6%)
  other arithmetic  5.11 us (3%)
    reduce_scatter x1, waiting for transfers between devices, per_device(): lax.psum_scatter(grads[2][None].astype(jnp.bfloat16), 'dp', scatter_dimen...  23.1 us
    all_to_all x1, waiting for transfers between devices, per_device(): lax.all_to_all(slot_grad.reshape(experts, capacity, width), 'expert', spl...  19.1 us
    all_to_all x1, starting transfers between devices, per_device(): lax.all_to_all(send_in, 'expert', split_axis=0, concat_axis=0, tiled=True)  17.4 us
    all_to_all x1, waiting for transfers between devices, per_device(): lax.all_to_all(slot_out.reshape(experts, capacity, width), 'expert', spli...  16.2 us
    all_gather x1, blocking collectives, per_device(): lax.all_gather(w_down, 'dp', axis=2, tiled=True)  14.3 us
    all_gather x1, blocking collectives, per_device(): lax.all_gather(w_gate, 'dp', axis=1, tiled=True)  14 us
    all_to_all x1, starting transfers between devices, per_device(): lax.all_to_all(slot_out.reshape(experts, capacity, width), 'expert', spli...  13.8 us
    all_gather x1, blocking collectives, per_device(): lax.all_gather(w_up, 'dp', axis=1, tiled=True)  13.7 us
  transfers between devices with their start and end apart: 7, of which 4 were waited for; matrix products, arithmetic and copies ran while one was open for 9% of the time, Pallas kernels for 0%

commit v1 on v0

v1 whole, which is shorter than its diff:
```python
import jax
import jax.numpy as jnp
from jax import lax
from jax.experimental import pallas as pl
from jax.experimental.pallas import tpu as pltpu
from jax.sharding import PartitionSpec as P

BF = jnp.bfloat16
F32 = jnp.float32
VMEM = pl.BlockSpec(memory_space=pltpu.VMEM)
SMEM = pl.BlockSpec(memory_space=pltpu.SMEM)


def mm(a, b):
    return lax.dot_general(a, b, (((1,), (0,)), ((), ())), preferred_element_type=F32)


def mm_nt(a, b):
    return lax.dot_general(a, b, (((1,), (1,)), ((), ())), preferred_element_type=F32)


def mm_tn(a, b):
    return lax.dot_general(a, b, (((0,), (0,)), ((), ())), preferred_element_type=F32)


def source_of(o):
    return ((o >> 1) & 15) * 16 + (o & 1) * 8 + (o >> 5)


def sorting():
    rows = lax.broadcasted_iota(jnp.int32, (256, 256), 0)
    cols = lax.broadcasted_iota(jnp.int32, (256, 256), 1)
    return jnp.where(source_of(rows) == cols, 1.0, 0.0).astype(BF)


def unsorting():
    rows = lax.broadcasted_iota(jnp.int32, (256, 256), 0)
    cols = lax.broadcasted_iota(jnp.int32, (256, 256), 1)
    return jnp.where(source_of(cols) == rows, 1.0, 0.0).astype(BF)


def pack_weights_kernel(wg, wu, wd, out):
    out[0:256, :] = wg[0, :, 0:256]
    out[256:512, :] = wu[0, :, 0:256]
    out[512:768, 0:128] = wg[0, :, 256:384]
    out[512:768, 128:256] = wu[0, :, 256:384]
    out[768:1152, :] = wd[0]


def columns_of(row):
    return jnp.transpose(jnp.broadcast_to(row, (128, 128)))


def pack_rows_kernel(ids, gates, x, cot, send, place):
    row_ids = ids[...].astype(F32)
    across = jnp.broadcast_to(row_ids, (128, 128))
    down = jnp.transpose(across)
    earlier = lax.broadcasted_iota(jnp.int32, (128, 128), 0) < lax.broadcasted_iota(
        jnp.int32, (128, 128), 1
    )
    rank = jnp.sum(jnp.where((across == down) & earlier, 1.0, 0.0), axis=0, keepdims=True)
    slot = (row_ids * 2.0 + rank).astype(jnp.int32)
    onehot = jnp.where(
        lax.broadcasted_iota(jnp.int32, (256, 128), 0) == slot, 1.0, 0.0
    ).astype(BF)
    place[...] = onehot
    gate = columns_of(gates[...])
    back = unsorting()
    pieces = []
    for piece in range(4):
        pieces.append(mm(onehot, x[:, piece * 256 : piece * 256 + 256]).astype(BF))
    for piece in range(4):
        lower = cot[:, piece * 256 : piece * 256 + 128].astype(F32) * gate
        upper = cot[:, piece * 256 + 128 : piece * 256 + 256].astype(F32) * gate
        scaled = jnp.concatenate([lower, upper], 1).astype(BF)
        pieces.append(mm(onehot, scaled).astype(BF))
    for b in range(8):
        block = jnp.concatenate([p[b * 32 : b * 32 + 32, :] for p in pieces], 0)
        send[b * 256 : b * 256 + 256, :] = mm(back, block).astype(BF)


def expert_kernel(index, recv, w0, w1, w2, w3, send, g0, g1, g2, g3, rows, outs):
    me = index[0]
    sort = sorting()
    for b in range(8):
        block = mm(sort, recv[b * 256 : b * 256 + 256, :]).astype(BF)
        for piece in range(8):
            rows[piece, b * 32 : b * 32 + 32, :] = block[piece * 32 : piece * 32 + 32, :]
    shards = (w0, w1, w2, w3)
    gate_lo = up_lo = both_hi = backed = None
    for k in range(4):
        w = shards[k]
        q = (me + 4 - k) & 3
        xq = rows[q]
        sq = rows[4 + q]
        terms = (
            mm(xq, w[0:256, :]),
            mm(xq, w[256:512, :]),
            mm(xq, w[512:768, :]),
            mm_nt(sq, w[768:1152, :]),
        )
        if k == 0:
            gate_lo, up_lo, both_hi, backed = terms
        else:
            gate_lo, up_lo, both_hi, backed = (
                gate_lo + terms[0],
                up_lo + terms[1],
                both_hi + terms[2],
                backed + terms[3],
            )
    gate_act = jnp.concatenate([gate_lo, both_hi[:, 0:128]], 1)
    up_act = jnp.concatenate([up_lo, both_hi[:, 128:256]], 1)
    sigma = jax.nn.sigmoid(gate_act)
    hidden = (gate_act * sigma * up_act).astype(BF)
    d_gate = (backed * up_act * sigma * (1.0 + gate_act * (1.0 - sigma))).astype(BF)
    d_up = (backed * gate_act * sigma).astype(BF)
    dg_lo = d_gate[:, 0:256]
    du_lo = d_up[:, 0:256]
    d_hi = jnp.concatenate([d_gate[:, 256:384], d_up[:, 256:384]], 1)
    for k in range(4):
        w = shards[k]
        q = (me + 4 - k) & 3
        outs[q] = mm(hidden, w[768:1152, :]).astype(BF)
        outs[4 + q] = (
            mm_nt(dg_lo, w[0:256, :]) + mm_nt(du_lo, w[256:512, :]) + mm_nt(d_hi, w[512:768, :])
        ).astype(BF)
    back = unsorting()
    for b in range(8):
        block = jnp.concatenate([outs[p, b * 32 : b * 32 + 32, :] for p in range(8)], 0)
        send[b * 256 : b * 256 + 256, :] = mm(back, block).astype(BF)
    for k, g in enumerate((g0, g1, g2, g3)):
        q = (me + k) & 3
        xq = rows[q]
        sq = rows[4 + q]
        g[0:256, :] = mm_tn(xq, dg_lo).astype(BF)
        g[256:512, :] = mm_tn(xq, du_lo).astype(BF)
        g[512:768, :] = mm_tn(xq, d_hi).astype(BF)
        g[768:1152, :] = mm_tn(hidden, sq).astype(BF)


def unpack_kernel(recv, place, gates, cot, gated_out, input_grad, gate_grad, flat):
    sort = sorting()
    for b in range(8):
        block = mm(sort, recv[b * 256 : b * 256 + 256, :]).astype(BF)
        for piece in range(8):
            flat[b * 32 : b * 32 + 32, piece * 256 : piece * 256 + 256] = block[
                piece * 32 : piece * 32 + 32, :
            ]
    onehot = place[...]
    gate = columns_of(gates[...])
    total = jnp.zeros((128, 128), F32)
    row_out = mm_tn(onehot, flat[:, 0:1024])
    for part in range(8):
        cols = slice(part * 128, part * 128 + 128)
        piece = row_out[:, cols]
        gated_out[:, cols] = (gate * piece).astype(BF)
        total = total + cot[:, cols].astype(F32) * piece
    gate_grad[...] = jnp.sum(jnp.transpose(total), axis=0, keepdims=True)
    input_grad[...] = mm_tn(onehot, flat[:, 1024:2048]).astype(BF)


def sum_kernel(g0, r1, r2, r3, out_gate, out_up, out_down):
    def total(rows):
        return (
            g0[rows, :].astype(F32)
            + r1[rows, :].astype(F32)
            + r2[rows, :].astype(F32)
            + r3[rows, :].astype(F32)
        ).astype(BF)

    out_gate[0, :, 0:256] = total(slice(0, 256))
    out_up[0, :, 0:256] = total(slice(256, 512))
    both = total(slice(512, 768))
    out_gate[0, :, 256:384] = both[:, 0:128]
    out_up[0, :, 256:384] = both[:, 128:256]
    out_down[0] = total(slice(768, 1152))


def call(kernel, name, outs, specs, flops, moved, scratch=(), limit=24 << 20):
    return pl.pallas_call(
        kernel,
        name=name,
        out_shape=[jax.ShapeDtypeStruct(s, d) for s, d in outs],
        in_specs=specs,
        out_specs=[VMEM] * len(outs),
        scratch_shapes=list(scratch),
        cost_estimate=pl.CostEstimate(flops=flops, bytes_accessed=moved, transcendentals=0),
        compiler_params=pltpu.CompilerParams(vmem_limit_bytes=limit),
    )


def pack_weights(wg, wu, wd):
    return call(
        pack_weights_kernel, "pack_weights", [((1152, 256), BF)], [VMEM] * 3, 0, 1200000
    )(wg, wu, wd)[0]


def pack_rows(ids, gates, x, cot):
    return call(
        pack_rows_kernel,
        "pack_rows",
        [((2048, 256), BF), ((256, 128), BF)],
        [VMEM] * 4,
        400000000,
        1600000,
    )(ids, gates, x, cot)


def expert_rows(index, recv, shards):
    return call(
        expert_kernel,
        "expert_rows",
        [((2048, 256), BF)] + [((1152, 256), BF)] * 4,
        [SMEM] + [VMEM] * 5,
        2400000000,
        7000000,
        [pltpu.VMEM((8, 256, 256), BF), pltpu.VMEM((8, 256, 256), BF)],
        40 << 20,
    )(index, recv, *shards)


def unpack_rows(recv, place, gates, cot):
    return call(
        unpack_kernel,
        "unpack_rows",
        [((128, 1024), BF), ((128, 1024), BF), ((1, 128), F32)],
        [VMEM] * 4,
        400000000,
        2000000,
        [pltpu.VMEM((256, 2048), BF)],
    )(recv, place, gates, cot)


def sum_grads(parts):
    return call(
        sum_kernel,
        "sum_grads",
        [((1, 256, 384), BF), ((1, 256, 384), BF), ((1, 384, 256), BF)],
        [VMEM] * 4,
        0,
        3000000,
    )(*parts)


def per_device(x_rows, expert_ids, gates, cotangent, w_gate, w_up, w_down):
    groups = lax.axis_size("dp")

    def shift(value, k):
        return lax.ppermute(value, "dp", [(i, (i + k) % groups) for i in range(groups)])

    def exchange(rows):
        wire = rows.reshape(128, 16, 256)
        moved = lax.all_to_all(wire, "expert", split_axis=0, concat_axis=0, tiled=True)
        return moved.reshape(2048, 256)

    ids = expert_ids.reshape(1, 128)
    gate_row = gates.reshape(1, 128)
    own = pack_weights(w_gate, w_up, w_down)
    shards = [own] + [shift(own, k) for k in (1, 2, 3)]
    send, place = pack_rows(ids, gate_row, x_rows, cotangent)
    recv = exchange(send)
    index = lax.axis_index("dp").astype(jnp.int32).reshape(1)
    out = expert_rows(index, recv, shards)
    returned = exchange(out[0])
    parts = [out[1]] + [shift(out[1 + k], k) for k in (1, 2, 3)]
    gated_out, input_grad, gate_grad = unpack_rows(returned, place, gate_row, cotangent)
    grads = sum_grads(parts)
    return (gated_out, input_grad, gate_grad.reshape(128, 1), *grads)


def solution(mesh):
    in_specs = (
        P(("dp", "expert"), None),
        P(("dp", "expert"), None),
        P(("dp", "expert"), None),
        P(("dp", "expert"), None),
        P("expert", "dp", None),
        P("expert", "dp", None),
        P("expert", None, "dp"),
    )
    out_specs = (
        P(("dp", "expert"), None),
        P(("dp", "expert"), None),
        P(("dp", "expert"), None),
        P("expert", "dp", None),
        P("expert", "dp", None),
        P("expert", None, "dp"),
    )
    return jax.shard_map(
        per_device, mesh=mesh, in_specs=in_specs, out_specs=out_specs, check_vma=False
    )
```

time: 195 us -> 117 us (0.60)
  the two profiles are of different devices: /device:TPU:8 before, /device:TPU:15 now
where the time goes in v1:
time: 117 us
  starting transfers between devices  50.4 us (43%)
  waiting for transfers between devices  50.4 us (43%)
  Pallas kernels  8.31 us (7%)
  local copies, waits for them, and re-layouts  6.92 us (6%)
    ppermute x6, waiting for transfers between devices, shift(): lax.ppermute(value, 'dp', [(i, (i + k) % groups) for i in range(groups)])  50.4 us
    all_to_all x2, starting transfers between devices, exchange(): lax.all_to_all(wire, 'expert', split_axis=0, concat_axis=0, tiled=True)  32.8 us
    ppermute x6, starting transfers between devices, shift(): lax.ppermute(value, 'dp', [(i, (i + k) % groups) for i in range(groups)])  17.6 us
    unnamed x32, local copies, waits for them, and re-layouts  6.92 us
    pallas_call x1, Pallas kernels, expert_rows(): call(expert_kernel, 'expert_rows', [((2048, 256), BF)] + [((1152, 256), B...  3.98 us
  transfers between devices with their start and end apart: 8, of which 5 were waited for; matrix products, arithmetic and copies ran while one was open for 0% of the time, Pallas kernels for 1%

profile of v1, /device:TPU:15, one launch (start us, length us, event | category | flops | bytes accessed | tf_op | source)
XLA Modules:
  0.0 116.8 jit_solution(12608248809530278372)
XLA Ops:
  0.6 0.0 copy-start.14
  0.6 0.0 copy-start.15
  0.7 0.6 copy-done.14
  1.3 0.0 copy-done.15
  1.3 0.9 copy-done.11
  2.3 0.9 copy-done.12
  3.2 1.9 %pack_rows.1 = (bf16[2048,256]{1,0:T(8,128)(2,1)}, bf16[256,128]{1,0:T(8,128)(2,1)S(1)}) custom-call(s32[1,128]{1,0:T(1,128)S(1)} %bitcast.10, f32[1,128]{1,0:T(1,128)S(1)} %bitcast.11, bf16[128,1024]{1,0:T(8,128)(2,1)S(1)} %copy-done.11, bf16[128,1024]{1,0:T(8,128)(2,1)S(1)} %copy-done.12), custom_call_target="tpu_custom_call" | custom-call | flops 400000000 | bytes 1600000 | tf_op jit(solution)/shard_map/pack_rows/pallas_call | solution.py:199
  5.1 17.8 %all-to-all-start = ((bf16[128,16,256]{2,1,0:T(8,128)(2,1)}), bf16[128,16,256]{2,1,0:T(8,128)(2,1)S(1)}, u32[]{:S(2)}, u32[]{:S(2)}) async-start(bf16[128,16,256]{2,1,0:T(8,128)(2,1)} %bitcast.3), calls=%async_computation | async-start | bytes 2097152 | tf_op jit(solution)/shard_map/all_to_all | solution.py:253
  22.9 0.1 pack_weights.1.w0
  23.0 2.5 %collective-permute-start.2 = (bf16[1152,256]{1,0:T(8,128)(2,1)S(1)}, bf16[1152,256]{1,0:T(8,128)(2,1)S(1)}, u32[]{:S(2)}, u32[]{:S(2)}) collective-permute-start(bf16[1152,256]{1,0:T(8,128)(2,1)S(1)} %pack_weights.1.w0), channel_id=1, source_target_pairs={{0,384},{128,0},{256,128},{384,256},{1,385},{129,1},{257,129},{385... | collective-permute-start | bytes 1769480 | tf_op jit(solution)/shard_map/ppermute | solution.py:249
  25.4 2.7 %collective-permute-start.1 = (bf16[1152,256]{1,0:T(8,128)(2,1)S(1)}, bf16[1152,256]{1,0:T(8,128)(2,1)S(1)}, u32[]{:S(2)}, u32[]{:S(2)}) collective-permute-start(bf16[1152,256]{1,0:T(8,128)(2,1)S(1)} %pack_weights.1.w0), channel_id=1, source_target_pairs={{0,256},{128,384},{256,0},{384,128},{1,257},{129,385},{257,1},{385... | collective-permute-start | bytes 1769480 | tf_op jit(solution)/shard_map/ppermute | solution.py:249
  28.2 3.7 %collective-permute-start = (bf16[1152,256]{1,0:T(8,128)(2,1)S(1)}, bf16[1152,256]{1,0:T(8,128)(2,1)S(1)}, u32[]{:S(2)}, u32[]{:S(2)}) collective-permute-start(bf16[1152,256]{1,0:T(8,128)(2,1)S(1)} %pack_weights.1.w0), channel_id=1, source_target_pairs={{0,128},{128,256},{256,384},{384,0},{1,129},{129,257},{257,385},{3... | collective-permute-start | bytes 1769480 | tf_op jit(solution)/shard_map/ppermute | solution.py:249
  31.9 21.3 %collective-permute-done.2.w3 = bf16[1152,256]{1,0:T(8,128)(2,1)S(1)} collective-permute-done((bf16[1152,256]{1,0:T(8,128)(2,1)S(1)}, bf16[1152,256]{1,0:T(8,128)(2,1)S(1)}, u32[]{:S(2)}, u32[]{:S(2)}) %collective-permute-start.2) | collective-permute-done | bytes 589856 | tf_op jit(solution)/shard_map/ppermute | solution.py:249
  53.2 0.0 collective-permute-done.1.w2
  53.2 2.3 %collective-permute-done.w1 = bf16[1152,256]{1,0:T(8,128)(2,1)S(1)} collective-permute-done((bf16[1152,256]{1,0:T(8,128)(2,1)S(1)}, bf16[1152,256]{1,0:T(8,128)(2,1)S(1)}, u32[]{:S(2)}, u32[]{:S(2)}) %collective-permute-start) | collective-permute-done | bytes 589856 | tf_op jit(solution)/shard_map/ppermute | solution.py:249
  55.5 0.8 copy-done.5
  56.3 0.0 all-to-all-done
  56.3 1.1 copy-done.6
  57.4 4.0 %expert_rows.1 = (bf16[2048,256]{1,0:T(8,128)(2,1)}, bf16[1152,256]{1,0:T(8,128)(2,1)S(1)}, bf16[1152,256]{1,0:T(8,128)(2,1)S(1)}, bf16[1152,256]{1,0:T(8,128)(2,1)S(1)}, bf16[1152,256]{1,0:T(8,128)(2,1)S(1)}) custom-call(s32[1]{0:T(128)} %bitcast.index, bf16[2048,256]{1,0:T(8,128)(2,1)S(1)} %bitcast.9, bf16[1152,256]{1,0:T(8,128)(2,1)S(1)} %pack_weights.1.w0, ...), custom_call_target="tpu_custom_call" | custom-call | flops 2400000000 | bytes 7000000 | tf_op jit(solution)/shard_map/expert_rows/pallas_call | solution.py:210
  61.4 0.8 copy-done.3
  62.2 0.8 copy-done.7
  63.0 0.8 copy-done.9
  63.8 15.0 %all-to-all-start.1 = ((bf16[128,16,256]{2,1,0:T(8,128)(2,1)}), bf16[128,16,256]{2,1,0:T(8,128)(2,1)S(1)}, u32[]{:S(2)}, u32[]{:S(2)}) async-start(bf16[128,16,256]{2,1,0:T(8,128)(2,1)} %bitcast.5), calls=%async_computation.1 | async-start | bytes 2097152 | tf_op jit(solution)/shard_map/all_to_all | solution.py:253
  78.8 4.3 %collective-permute-start.3 = (bf16[1152,256]{1,0:T(8,128)(2,1)S(1)}, bf16[1152,256]{1,0:T(8,128)(2,1)S(1)}, u32[]{:S(2)}, u32[]{:S(2)}) collective-permute-start(bf16[1152,256]{1,0:T(8,128)(2,1)S(1)} %copy-done.10), channel_id=1, source_target_pairs={{0,128},{128,256},{256,384},{384,0},{1,129},{129,257},{257,385},{3... | collective-permute-start | bytes 1769480 | tf_op jit(solution)/shard_map/ppermute | solution.py:249
  83.1 1.9 %collective-permute-start.4 = (bf16[1152,256]{1,0:T(8,128)(2,1)S(1)}, bf16[1152,256]{1,0:T(8,128)(2,1)S(1)}, u32[]{:S(2)}, u32[]{:S(2)}) collective-permute-start(bf16[1152,256]{1,0:T(8,128)(2,1)S(1)} %copy-done.8), channel_id=1, source_target_pairs={{0,256},{128,384},{256,0},{384,128},{1,257},{129,385},{257,1},{385... | collective-permute-start | bytes 1769480 | tf_op jit(solution)/shard_map/ppermute | solution.py:249
  85.0 2.5 %collective-permute-start.5 = (bf16[1152,256]{1,0:T(8,128)(2,1)S(1)}, bf16[1152,256]{1,0:T(8,128)(2,1)S(1)}, u32[]{:S(2)}, u32[]{:S(2)}) collective-permute-start(bf16[1152,256]{1,0:T(8,128)(2,1)S(1)} %copy-done.4), channel_id=1, source_target_pairs={{0,384},{128,0},{256,128},{384,256},{1,385},{129,1},{257,129},{385... | collective-permute-start | bytes 1769480 | tf_op jit(solution)/shard_map/ppermute | solution.py:249
  87.5 8.5 %collective-permute-done.3.r1 = bf16[1152,256]{1,0:T(8,128)(2,1)S(1)} collective-permute-done((bf16[1152,256]{1,0:T(8,128)(2,1)S(1)}, bf16[1152,256]{1,0:T(8,128)(2,1)S(1)}, u32[]{:S(2)}, u32[]{:S(2)}) %collective-permute-start.3) | collective-permute-done | bytes 589856 | tf_op jit(solution)/shard_map/ppermute | solution.py:249
  96.0 4.7 %collective-permute-done.4.r2 = bf16[1152,256]{1,0:T(8,128)(2,1)S(1)} collective-permute-done((bf16[1152,256]{1,0:T(8,128)(2,1)S(1)}, bf16[1152,256]{1,0:T(8,128)(2,1)S(1)}, u32[]{:S(2)}, u32[]{:S(2)}) %collective-permute-start.4) | collective-permute-done | bytes 589856 | tf_op jit(solution)/shard_map/ppermute | solution.py:249
  100.8 13.6 %collective-permute-done.5.r3 = bf16[1152,256]{1,0:T(8,128)(2,1)S(1)} collective-permute-done((bf16[1152,256]{1,0:T(8,128)(2,1)S(1)}, bf16[1152,256]{1,0:T(8,128)(2,1)S(1)}, u32[]{:S(2)}, u32[]{:S(2)}) %collective-permute-start.5) | collective-permute-done | bytes 589856 | tf_op jit(solution)/shard_map/ppermute | solution.py:249
  114.4 1.0 sum_grads.1
  115.4 0.0 all-to-all-done.1
  115.4 1.4 %unpack_rows.1 = (bf16[128,1024]{1,0:T(8,128)(2,1)}, bf16[128,1024]{1,0:T(8,128)(2,1)}, f32[1,128]{1,0:T(1,128)}) custom-call(bf16[2048,256]{1,0:T(8,128)(2,1)S(1)} %bitcast.8, bf16[256,128]{1,0:T(8,128)(2,1)S(1)} %get-tuple-element.21.place, f32[1,128]{1,0:T(1,128)S(1)} %bitcast.12, bf16[128,1024]{1,0:T(8,128)(2,1)S(1)} %copy-done.13), custom_call_target="tpu_custom_call" | custom-call | flops 400000000 | bytes 2000000 | tf_op jit(solution)/shard_map/unpack_rows/pallas_call | solution.py:223
  (21 shorter events, 0.0 us)
Async XLA Ops:
  0.6 0.7 copy-start.14
  0.6 0.7 copy-start.15
  1.3 0.9 copy-start.11
  2.3 0.9 copy-start.12
  5.1 17.8 %copy-start = (bf16[1,256,384]{2,1,0:T(8,128)(2,1)S(1)}, bf16[1,256,384]{2,1,0:T(8,128)(2,1)}, u32[]{:S(2)}) copy-start(bf16[1,256,384]{2,1,0:T(8,128)(2,1)} %wg.1) | copy-start | bytes 589828
  5.1 17.8 %copy-start.1 = (bf16[1,256,384]{2,1,0:T(8,128)(2,1)S(1)}, bf16[1,256,384]{2,1,0:T(8,128)(2,1)}, u32[]{:S(2)}) copy-start(bf16[1,256,384]{2,1,0:T(8,128)(2,1)} %wu.1) | copy-start | bytes 589828
  5.1 17.8 %copy-start.2 = (bf16[1,384,256]{2,1,0:T(8,128)(2,1)S(1)}, bf16[1,384,256]{2,1,0:T(8,128)(2,1)}, u32[]{:S(2)}) copy-start(bf16[1,384,256]{2,1,0:T(8,128)(2,1)} %wd.1) | copy-start | bytes 589828
  5.1 51.2 %all-to-all-start = ((bf16[128,16,256]{2,1,0:T(8,128)(2,1)}), bf16[128,16,256]{2,1,0:T(8,128)(2,1)S(1)}, u32[]{:S(2)}, u32[]{:S(2)}) async-start(bf16[128,16,256]{2,1,0:T(8,128)(2,1)} %bitcast.3), calls=%async_computation | async-start | bytes 2097152 | tf_op jit(solution)/shard_map/all_to_all | solution.py:253
  23.0 30.2 %collective-permute-start.2 = (bf16[1152,256]{1,0:T(8,128)(2,1)S(1)}, bf16[1152,256]{1,0:T(8,128)(2,1)S(1)}, u32[]{:S(2)}, u32[]{:S(2)}) collective-permute-start(bf16[1152,256]{1,0:T(8,128)(2,1)S(1)} %pack_weights.1.w0), channel_id=1, source_target_pairs={{0,384},{128,0},{256,128},{384,256},{1,385},{129,1},{257,129},{385... | collective-permute-start | bytes 1769480 | tf_op jit(solution)/shard_map/ppermute | solution.py:249
  25.4 27.8 %collective-permute-start.1 = (bf16[1152,256]{1,0:T(8,128)(2,1)S(1)}, bf16[1152,256]{1,0:T(8,128)(2,1)S(1)}, u32[]{:S(2)}, u32[]{:S(2)}) collective-permute-start(bf16[1152,256]{1,0:T(8,128)(2,1)S(1)} %pack_weights.1.w0), channel_id=1, source_target_pairs={{0,256},{128,384},{256,0},{384,128},{1,257},{129,385},{257,1},{385... | collective-permute-start | bytes 1769480 | tf_op jit(solution)/shard_map/ppermute | solution.py:249
  28.2 27.3 %collective-permute-start = (bf16[1152,256]{1,0:T(8,128)(2,1)S(1)}, bf16[1152,256]{1,0:T(8,128)(2,1)S(1)}, u32[]{:S(2)}, u32[]{:S(2)}) collective-permute-start(bf16[1152,256]{1,0:T(8,128)(2,1)S(1)} %pack_weights.1.w0), channel_id=1, source_target_pairs={{0,128},{128,256},{256,384},{384,0},{1,129},{129,257},{257,385},{3... | collective-permute-start | bytes 1769480 | tf_op jit(solution)/shard_map/ppermute | solution.py:249
  55.5 0.8 copy-start.5
  56.3 1.1 copy-start.6
  61.3 0.8 copy-start.3
  62.2 0.8 copy-start.7
  63.0 0.8 copy-start.9
  63.8 15.0 %copy-start.10 = (bf16[1152,256]{1,0:T(8,128)(2,1)S(1)}, bf16[1152,256]{1,0:T(8,128)(2,1)}, u32[]{:S(2)}) copy-start(bf16[1152,256]{1,0:T(8,128)(2,1)} %copy-done.9) | copy-start | bytes 1769476
  63.8 19.3 %copy-start.8 = (bf16[1152,256]{1,0:T(8,128)(2,1)S(1)}, bf16[1152,256]{1,0:T(8,128)(2,1)}, u32[]{:S(2)}) copy-start(bf16[1152,256]{1,0:T(8,128)(2,1)} %copy-done.7) | copy-start | bytes 1769476
  63.8 21.2 %copy-start.4 = (bf16[1152,256]{1,0:T(8,128)(2,1)S(1)}, bf16[1152,256]{1,0:T(8,128)(2,1)}, u32[]{:S(2)}) copy-start(bf16[1152,256]{1,0:T(8,128)(2,1)} %copy-done.3) | copy-start | bytes 1769476
  63.8 51.6 %all-to-all-start.1 = ((bf16[128,16,256]{2,1,0:T(8,128)(2,1)}), bf16[128,16,256]{2,1,0:T(8,128)(2,1)S(1)}, u32[]{:S(2)}, u32[]{:S(2)}) async-start(bf16[128,16,256]{2,1,0:T(8,128)(2,1)} %bitcast.5), calls=%async_computation.1 | async-start | bytes 2097152 | tf_op jit(solution)/shard_map/all_to_all | solution.py:253
  78.8 17.2 %collective-permute-start.3 = (bf16[1152,256]{1,0:T(8,128)(2,1)S(1)}, bf16[1152,256]{1,0:T(8,128)(2,1)S(1)}, u32[]{:S(2)}, u32[]{:S(2)}) collective-permute-start(bf16[1152,256]{1,0:T(8,128)(2,1)S(1)} %copy-done.10), channel_id=1, source_target_pairs={{0,128},{128,256},{256,384},{384,0},{1,129},{129,257},{257,385},{3... | collective-permute-start | bytes 1769480 | tf_op jit(solution)/shard_map/ppermute | solution.py:249
  83.1 17.7 %collective-permute-start.4 = (bf16[1152,256]{1,0:T(8,128)(2,1)S(1)}, bf16[1152,256]{1,0:T(8,128)(2,1)S(1)}, u32[]{:S(2)}, u32[]{:S(2)}) collective-permute-start(bf16[1152,256]{1,0:T(8,128)(2,1)S(1)} %copy-done.8), channel_id=1, source_target_pairs={{0,256},{128,384},{256,0},{384,128},{1,257},{129,385},{257,1},{385... | collective-permute-start | bytes 1769480 | tf_op jit(solution)/shard_map/ppermute | solution.py:249
  85.0 29.3 %collective-permute-start.5 = (bf16[1152,256]{1,0:T(8,128)(2,1)S(1)}, bf16[1152,256]{1,0:T(8,128)(2,1)S(1)}, u32[]{:S(2)}, u32[]{:S(2)}) collective-permute-start(bf16[1152,256]{1,0:T(8,128)(2,1)S(1)} %copy-done.4), channel_id=1, source_target_pairs={{0,384},{128,0},{256,128},{384,256},{1,385},{129,1},{257,129},{385... | collective-permute-start | bytes 1769480 | tf_op jit(solution)/shard_map/ppermute | solution.py:249
  114.4 1.0 copy-start.13

commit v2 on v1

--- a/solution.py
+++ b/solution.py
@@ -5,10 +5,12 @@
 from jax.experimental.pallas import tpu as pltpu
 from jax.sharding import PartitionSpec as P
 
+
 BF = jnp.bfloat16
 F32 = jnp.float32
 VMEM = pl.BlockSpec(memory_space=pltpu.VMEM)
 SMEM = pl.BlockSpec(memory_space=pltpu.SMEM)
+HBM = pl.BlockSpec(memory_space=pltpu.HBM)
 
 
 def mm(a, b):
@@ -39,20 +41,38 @@
     return jnp.where(source_of(cols) == rows, 1.0, 0.0).astype(BF)
 
 
-def pack_weights_kernel(wg, wu, wd, out):
-    out[0:256, :] = wg[0, :, 0:256]
-    out[256:512, :] = wu[0, :, 0:256]
-    out[512:768, 0:128] = wg[0, :, 256:384]
-    out[512:768, 128:256] = wu[0, :, 256:384]
-    out[768:1152, :] = wd[0]
-
-
 def columns_of(row):
     return jnp.transpose(jnp.broadcast_to(row, (128, 128)))
 
 
-def pack_rows_kernel(ids, gates, x, cot, send, place):
-    row_ids = ids[...].astype(F32)
+def weight_copies(wg, wu, wd, out, sems):
+    return (
+        pltpu.make_async_copy(wg.at[0, :, 0:256], out.at[0:256, :], sems.at[0]),
+        pltpu.make_async_copy(wu.at[0, :, 0:256], out.at[256:512, :], sems.at[1]),
+        pltpu.make_async_copy(wg.at[0, :, 256:384], out.at[512:768, 0:128], sems.at[2]),
+        pltpu.make_async_copy(wu.at[0, :, 256:384], out.at[512:768, 128:256], sems.at[3]),
+        pltpu.make_async_copy(wd.at[0], out.at[768:1152, :], sems.at[4]),
+    )
+
+
+def pack_kernel(
+    ids, gates, x, cot, wg, wu, wd, own, send, place, ids_v, gates_v, x_v, cot_v, send_v, sems, out_sems
+):
+    small = (
+        pltpu.make_async_copy(ids, ids_v, sems.at[5]),
+        pltpu.make_async_copy(gates, gates_v, sems.at[6]),
+    )
+    large = (
+        pltpu.make_async_copy(x, x_v, sems.at[7]),
+        pltpu.make_async_copy(cot, cot_v, sems.at[8]),
+    )
+    weights = weight_copies(wg, wu, wd, own, sems)
+    for copy in small + large + weights:
+        copy.start()
+    back = unsorting()
+    for copy in small:
+        copy.wait()
+    row_ids = ids_v[...].astype(F32)
     across = jnp.broadcast_to(row_ids, (128, 128))
     down = jnp.transpose(across)
     earlier = lax.broadcasted_iota(jnp.int32, (128, 128), 0) < lax.broadcasted_iota(
@@ -64,40 +84,58 @@
         lax.broadcasted_iota(jnp.int32, (256, 128), 0) == slot, 1.0, 0.0
     ).astype(BF)
     place[...] = onehot
-    gate = columns_of(gates[...])
-    back = unsorting()
+    gate = columns_of(gates_v[...])
     pieces = []
+    large[0].wait()
     for piece in range(4):
-        pieces.append(mm(onehot, x[:, piece * 256 : piece * 256 + 256]).astype(BF))
+        pieces.append(mm(onehot, x_v[:, piece * 256 : piece * 256 + 256]).astype(BF))
+    large[1].wait()
     for piece in range(4):
-        lower = cot[:, piece * 256 : piece * 256 + 128].astype(F32) * gate
-        upper = cot[:, piece * 256 + 128 : piece * 256 + 256].astype(F32) * gate
+        lower = cot_v[:, piece * 256 : piece * 256 + 128].astype(F32) * gate
+        upper = cot_v[:, piece * 256 + 128 : piece * 256 + 256].astype(F32) * gate
         scaled = jnp.concatenate([lower, upper], 1).astype(BF)
         pieces.append(mm(onehot, scaled).astype(BF))
+    leaving = []
     for b in range(8):
         block = jnp.concatenate([p[b * 32 : b * 32 + 32, :] for p in pieces], 0)
-        send[b * 256 : b * 256 + 256, :] = mm(back, block).astype(BF)
-
-
-def expert_kernel(index, recv, w0, w1, w2, w3, send, g0, g1, g2, g3, rows, outs):
+        rows = pl.ds(b * 256, 256)
+        send_v[rows, :] = mm(back, block).astype(BF)
+        leaving.append(pltpu.make_async_copy(send_v.at[rows, :], send.at[rows, :], out_sems.at[b]))
+        leaving[-1].start()
+    for copy in weights:
+        copy.wait()
+    for copy in leaving:
+        copy.wait()
+
+
+def expert_kernel(
+    index, recv, wg, wu, wd, w1, w2, w3, send, g0, g1, g2, g3,
+    rows, outs, shards, send_v, grads_v, own_sems, in_sems, out_sems, grad_sems,
+):
     me = index[0]
+    arriving = [weight_copies(wg, wu, wd, shards.at[0], own_sems)]
+    for k, w in enumerate((w1, w2, w3)):
+        arriving.append((pltpu.make_async_copy(w, shards.at[k + 1], in_sems.at[k]),))
+    for copies in arriving:
+        for copy in copies:
+            copy.start()
     sort = sorting()
     for b in range(8):
         block = mm(sort, recv[b * 256 : b * 256 + 256, :]).astype(BF)
         for piece in range(8):
             rows[piece, b * 32 : b * 32 + 32, :] = block[piece * 32 : piece * 32 + 32, :]
-    shards = (w0, w1, w2, w3)
     gate_lo = up_lo = both_hi = backed = None
     for k in range(4):
-        w = shards[k]
+        for copy in arriving[k]:
+            copy.wait()
         q = (me + 4 - k) & 3
         xq = rows[q]
         sq = rows[4 + q]
         terms = (
-            mm(xq, w[0:256, :]),
-            mm(xq, w[256:512, :]),
-            mm(xq, w[512:768, :]),
-            mm_nt(sq, w[768:1152, :]),
+            mm(xq, shards[k, 0:256, :]),
+            mm(xq, shards[k, 256:512, :]),
+            mm(xq, shards[k, 512:768, :]),
+            mm_nt(sq, shards[k, 768:1152, :]),
         )
         if k == 0:
             gate_lo, up_lo, both_hi, backed = terms
@@ -118,24 +156,33 @@
     du_lo = d_up[:, 0:256]
     d_hi = jnp.concatenate([d_gate[:, 256:384], d_up[:, 256:384]], 1)
     for k in range(4):
-        w = shards[k]
         q = (me + 4 - k) & 3
-        outs[q] = mm(hidden, w[768:1152, :]).astype(BF)
+        outs[q] = mm(hidden, shards[k, 768:1152, :]).astype(BF)
         outs[4 + q] = (
-            mm_nt(dg_lo, w[0:256, :]) + mm_nt(du_lo, w[256:512, :]) + mm_nt(d_hi, w[512:768, :])
+            mm_nt(dg_lo, shards[k, 0:256, :])
+            + mm_nt(du_lo, shards[k, 256:512, :])
+            + mm_nt(d_hi, shards[k, 512:768, :])
         ).astype(BF)
     back = unsorting()
+    leaving = []
     for b in range(8):
         block = jnp.concatenate([outs[p, b * 32 : b * 32 + 32, :] for p in range(8)], 0)
-        send[b * 256 : b * 256 + 256, :] = mm(back, block).astype(BF)
-    for k, g in enumerate((g0, g1, g2, g3)):
+        part = pl.ds(b * 256, 256)
+        send_v[part, :] = mm(back, block).astype(BF)
+        leaving.append(pltpu.make_async_copy(send_v.at[part, :], send.at[part, :], out_sems.at[b]))
+        leaving[-1].start()
+    for k, g in ((2, g2), (1, g1), (3, g3), (0, g0)):
         q = (me + k) & 3
         xq = rows[q]
         sq = rows[4 + q]
-        g[0:256, :] = mm_tn(xq, dg_lo).astype(BF)
-        g[256:512, :] = mm_tn(xq, du_lo).astype(BF)
-        g[512:768, :] = mm_tn(xq, d_hi).astype(BF)
-        g[768:1152, :] = mm_tn(hidden, sq).astype(BF)
+        grads_v[k, 0:256, :] = mm_tn(xq, dg_lo).astype(BF)
+        grads_v[k, 256:512, :] = mm_tn(xq, du_lo).astype(BF)
+        grads_v[k, 512:768, :] = mm_tn(xq, d_hi).astype(BF)
+        grads_v[k, 768:1152, :] = mm_tn(hidden, sq).astype(BF)
+        leaving.append(pltpu.make_async_copy(grads_v.at[k], g, grad_sems.at[k]))
+        leaving[-1].start()
+    for copy in leaving:
+        copy.wait()
 
 
 def unpack_kernel(recv, place, gates, cot, gated_out, input_grad, gate_grad, flat):
@@ -176,55 +223,71 @@
     out_down[0] = total(slice(768, 1152))
 
 
-def call(kernel, name, outs, specs, flops, moved, scratch=(), limit=24 << 20):
+def call(kernel, outs, specs, out_specs, flops, moved, scratch=(), limit=12 << 20):
     return pl.pallas_call(
         kernel,
-        name=name,
         out_shape=[jax.ShapeDtypeStruct(s, d) for s, d in outs],
         in_specs=specs,
-        out_specs=[VMEM] * len(outs),
+        out_specs=out_specs,
         scratch_shapes=list(scratch),
         cost_estimate=pl.CostEstimate(flops=flops, bytes_accessed=moved, transcendentals=0),
         compiler_params=pltpu.CompilerParams(vmem_limit_bytes=limit),
     )
 
 
-def pack_weights(wg, wu, wd):
+def hbm(x):
+    return pltpu.with_memory_space_constraint(x, pltpu.HBM)
+
+
+def pack(ids, gates, x, cot, wg, wu, wd):
     return call(
-        pack_weights_kernel, "pack_weights", [((1152, 256), BF)], [VMEM] * 3, 0, 1200000
-    )(wg, wu, wd)[0]
-
-
-def pack_rows(ids, gates, x, cot):
-    return call(
-        pack_rows_kernel,
-        "pack_rows",
-        [((2048, 256), BF), ((256, 128), BF)],
-        [VMEM] * 4,
+        pack_kernel,
+        [((1152, 256), BF), ((2048, 256), BF), ((256, 128), BF)],
+        [HBM] * 7,
+        [VMEM, HBM, VMEM],
         400000000,
-        1600000,
-    )(ids, gates, x, cot)
-
-
-def expert_rows(index, recv, shards):
+        2600000,
+        [
+            pltpu.VMEM((1, 128), jnp.int32),
+            pltpu.VMEM((1, 128), F32),
+            pltpu.VMEM((128, 1024), BF),
+            pltpu.VMEM((128, 1024), BF),
+            pltpu.VMEM((2048, 256), BF),
+            pltpu.SemaphoreType.DMA((9,)),
+            pltpu.SemaphoreType.DMA((8,)),
+        ],
+    )(*map(hbm, (ids, gates, x, cot, wg, wu, wd)))
+
+
+def expert_rows(index, recv, wg, wu, wd, shards):
     return call(
         expert_kernel,
-        "expert_rows",
         [((2048, 256), BF)] + [((1152, 256), BF)] * 4,
-        [SMEM] + [VMEM] * 5,
+        [SMEM, VMEM] + [HBM] * 6,
+        [HBM] * 5,
         2400000000,
         7000000,
-        [pltpu.VMEM((8, 256, 256), BF), pltpu.VMEM((8, 256, 256), BF)],
-        40 << 20,
-    )(index, recv, *shards)
+        [
+            pltpu.VMEM((8, 256, 256), BF),
+            pltpu.VMEM((8, 256, 256), BF),
+            pltpu.VMEM((4, 1152, 256), BF),
+            pltpu.VMEM((2048, 256), BF),
+            pltpu.VMEM((4, 1152, 256), BF),
+            pltpu.SemaphoreType.DMA((5,)),
+            pltpu.SemaphoreType.DMA((3,)),
+            pltpu.SemaphoreType.DMA((8,)),
+            pltpu.SemaphoreType.DMA((4,)),
+        ],
+        24 << 20,
+    )(index, recv, *map(hbm, (wg, wu, wd, *shards)))
 
 
 def unpack_rows(recv, place, gates, cot):
     return call(
         unpack_kernel,
-        "unpack_rows",
         [((128, 1024), BF), ((128, 1024), BF), ((1, 128), F32)],
         [VMEM] * 4,
+        [VMEM] * 3,
         400000000,
         2000000,
         [pltpu.VMEM((256, 2048), BF)],
@@ -234,9 +297,9 @@
 def sum_grads(parts):
     return call(
         sum_kernel,
-        "sum_grads",
         [((1, 256, 384), BF), ((1, 256, 384), BF), ((1, 384, 256), BF)],
         [VMEM] * 4,
+        [VMEM] * 3,
         0,
         3000000,
     )(*parts)
@@ -255,14 +318,17 @@
 
     ids = expert_ids.reshape(1, 128)
     gate_row = gates.reshape(1, 128)
-    own = pack_weights(w_gate, w_up, w_down)
-    shards = [own] + [shift(own, k) for k in (1, 2, 3)]
-    send, place = pack_rows(ids, gate_row, x_rows, cotangent)
+    own, send, place = pack(ids, gate_row, x_rows, cotangent, w_gate, w_up, w_down)
+    shards = []
+    for k in (1, 2, 3):
+        shards.append(shift(own, k))
     recv = exchange(send)
     index = lax.axis_index("dp").astype(jnp.int32).reshape(1)
-    out = expert_rows(index, recv, shards)
+    out = expert_rows(index, recv, w_gate, w_up, w_down, shards)
     returned = exchange(out[0])
-    parts = [out[1]] + [shift(out[1 + k], k) for k in (1, 2, 3)]
+    parts = [out[1]]
+    for k in (1, 2, 3):
+        parts.append(shift(out[1 + k], k))
     gated_out, input_grad, gate_grad = unpack_rows(returned, place, gate_row, cotangent)
     grads = sum_grads(parts)
     return (gated_out, input_grad, gate_grad.reshape(128, 1), *grads)

time: 117 us -> 115 us (0.983)
  local copies, waits for them, and re-layouts: 6.92 us -> 1.48 us
  Pallas kernels: 8.31 us -> 11.3 us
    unnamed x32 -> x10, local copies, waits for them, and re-layouts: 6.92 us -> 1.48 us
    pallas_call x5 -> x4, Pallas kernels: 8.31 us -> 11.3 us  [the longest x1 6.05 us: expert_rows(): call(expert_kernel, [((2048, 256), BF)] + [((1152, 256), BF)] * 4, [SMEM,...]
where the time goes in v2:
time: 115 us; the launch traced here: 114 us
  waiting for transfers between devices  50.4 us (44%)
  starting transfers between devices  50.1 us (44%)
  Pallas kernels  11.3 us (10%)
  local copies, waits for them, and re-layouts  1.48 us (1%)
    ppermute x6, waiting for transfers between devices, shift(): lax.ppermute(value, 'dp', [(i, (i + k) % groups) for i in range(groups)])  50.4 us
    all_to_all x2, starting transfers between devices, exchange(): lax.all_to_all(wire, 'expert', split_axis=0, concat_axis=0, tiled=True)  32.5 us
    ppermute x6, starting transfers between devices, shift(): lax.ppermute(value, 'dp', [(i, (i + k) % groups) for i in range(groups)])  17.6 us
    pallas_call x1, Pallas kernels, expert_rows(): call(expert_kernel, [((2048, 256), BF)] + [((1152, 256), BF)] * 4, [SMEM,...  6.05 us
    pallas_call x1, Pallas kernels, pack(): call(pack_kernel, [((1152, 256), BF), ((2048, 256), BF), ((256, 128), BF)...  2.84 us
  transfers between devices with their start and end apart: 8, of which 5 were waited for; matrix products, arithmetic and copies ran while one was open for 0% of the time, Pallas kernels for 1%

profile of v2, /device:TPU:15, one launch (start us, length us, event | category | flops | bytes accessed | tf_op | source)
XLA Modules:
  0.0 114.0 jit_solution(16446664741364062524)
XLA Ops:
  0.6 2.8 %shard_map.118 = (bf16[1152,256]{1,0:T(8,128)(2,1)S(1)}, bf16[2048,256]{1,0:T(8,128)(2,1)}, bf16[256,128]{1,0:T(8,128)(2,1)S(1)}) custom-call(s32[1,128]{1,0:T(1,128)} %bitcast.12, f32[1,128]{1,0:T(1,128)} %bitcast.10, bf16[128,1024]{1,0:T(8,128)(2,1)} %x.1, bf16[128,1024]{1,0:T(8,128)(2,1)} %cot.3, bf16[1,256,384]{2,1,0:T(8,128)(2,1)} %wg.3, ...), custom_call_target="tpu_custom_call" | custom-call | flops 400000000 | bytes 2600000 | tf_op jit(solution)/shard_map/pallas_call | solution.py:243
  3.5 17.7 %all-to-all-start = ((bf16[128,16,256]{2,1,0:T(8,128)(2,1)}), bf16[128,16,256]{2,1,0:T(8,128)(2,1)S(1)}, u32[]{:S(2)}, u32[]{:S(2)}) async-start(bf16[128,16,256]{2,1,0:T(8,128)(2,1)} %bitcast.3), calls=%async_computation | async-start | bytes 2097152 | tf_op jit(solution)/shard_map/all_to_all | solution.py:316
  21.1 2.5 %collective-permute-start.2 = (bf16[1152,256]{1,0:T(8,128)(2,1)S(1)}, bf16[1152,256]{1,0:T(8,128)(2,1)S(1)}, u32[]{:S(2)}, u32[]{:S(2)}) collective-permute-start(bf16[1152,256]{1,0:T(8,128)(2,1)S(1)} %get-tuple-element.21), channel_id=1, source_target_pairs={{0,384},{128,0},{256,128},{384,256},{1,385},{129,1},{257,129},{385... | collective-permute-start | bytes 1769480 | tf_op jit(solution)/shard_map/ppermute | solution.py:312
  23.6 2.7 %collective-permute-start.1 = (bf16[1152,256]{1,0:T(8,128)(2,1)S(1)}, bf16[1152,256]{1,0:T(8,128)(2,1)S(1)}, u32[]{:S(2)}, u32[]{:S(2)}) collective-permute-start(bf16[1152,256]{1,0:T(8,128)(2,1)S(1)} %get-tuple-element.21), channel_id=1, source_target_pairs={{0,256},{128,384},{256,0},{384,128},{1,257},{129,385},{257,1},{385... | collective-permute-start | bytes 1769480 | tf_op jit(solution)/shard_map/ppermute | solution.py:312
  26.4 3.7 %collective-permute-start = (bf16[1152,256]{1,0:T(8,128)(2,1)S(1)}, bf16[1152,256]{1,0:T(8,128)(2,1)S(1)}, u32[]{:S(2)}, u32[]{:S(2)}) collective-permute-start(bf16[1152,256]{1,0:T(8,128)(2,1)S(1)} %get-tuple-element.21), channel_id=1, source_target_pairs={{0,128},{128,256},{256,384},{384,0},{1,129},{129,257},{257,385},{3... | collective-permute-start | bytes 1769480 | tf_op jit(solution)/shard_map/ppermute | solution.py:312
  30.1 21.3 %collective-permute-done.2.w3 = bf16[1152,256]{1,0:T(8,128)(2,1)S(1)} collective-permute-done((bf16[1152,256]{1,0:T(8,128)(2,1)S(1)}, bf16[1152,256]{1,0:T(8,128)(2,1)S(1)}, u32[]{:S(2)}, u32[]{:S(2)}) %collective-permute-start.2) | collective-permute-done | bytes 589856 | tf_op jit(solution)/shard_map/ppermute | solution.py:312
  51.4 0.0 copy-start.2
  51.4 0.0 collective-permute-done.1.w2
  51.4 0.0 copy-start.3
  51.4 2.2 %collective-permute-done.w1 = bf16[1152,256]{1,0:T(8,128)(2,1)S(1)} collective-permute-done((bf16[1152,256]{1,0:T(8,128)(2,1)S(1)}, bf16[1152,256]{1,0:T(8,128)(2,1)S(1)}, u32[]{:S(2)}, u32[]{:S(2)}) %collective-permute-start) | collective-permute-done | bytes 589856 | tf_op jit(solution)/shard_map/ppermute | solution.py:312
  53.6 0.0 copy-start.4
  53.6 0.0 all-to-all-done
  53.6 0.0 copy-done.2
  53.6 0.0 copy-done.3
  53.7 0.8 copy-done.4
  54.5 6.1 %shard_map.119 = (bf16[2048,256]{1,0:T(8,128)(2,1)}, bf16[1152,256]{1,0:T(8,128)(2,1)S(1)}, bf16[1152,256]{1,0:T(8,128)(2,1)S(1)}, bf16[1152,256]{1,0:T(8,128)(2,1)S(1)}, bf16[1152,256]{1,0:T(8,128)(2,1)S(1)}) custom-call(s32[1]{0:T(128)} %bitcast.index, bf16[2048,256]{1,0:T(8,128)(2,1)S(1)} %bitcast.9, bf16[1,256,384]{2,1,0:T(8,128)(2,1)} %wg.3, ...), custom_call_target="tpu_custom_call" | custom-call | flops 2400000000 | bytes 7000000 | tf_op jit(solution)/shard_map/pallas_call | solution.py:263
  60.5 14.9 %all-to-all-start.1 = ((bf16[128,16,256]{2,1,0:T(8,128)(2,1)}), bf16[128,16,256]{2,1,0:T(8,128)(2,1)S(1)}, u32[]{:S(2)}, u32[]{:S(2)}) async-start(bf16[128,16,256]{2,1,0:T(8,128)(2,1)} %bitcast.5), calls=%async_computation.1 | async-start | bytes 2097152 | tf_op jit(solution)/shard_map/all_to_all | solution.py:316
  75.4 4.3 %collective-permute-start.3 = (bf16[1152,256]{1,0:T(8,128)(2,1)S(1)}, bf16[1152,256]{1,0:T(8,128)(2,1)S(1)}, u32[]{:S(2)}, u32[]{:S(2)}) collective-permute-start(bf16[1152,256]{1,0:T(8,128)(2,1)S(1)} %get-tuple-element.28), channel_id=1, source_target_pairs={{0,128},{128,256},{256,384},{384,0},{1,129},{129,257},{257,385},{3... | collective-permute-start | bytes 1769480 | tf_op jit(solution)/shard_map/ppermute | solution.py:312
  79.7 1.9 %collective-permute-start.4 = (bf16[1152,256]{1,0:T(8,128)(2,1)S(1)}, bf16[1152,256]{1,0:T(8,128)(2,1)S(1)}, u32[]{:S(2)}, u32[]{:S(2)}) collective-permute-start(bf16[1152,256]{1,0:T(8,128)(2,1)S(1)} %get-tuple-element.29), channel_id=1, source_target_pairs={{0,256},{128,384},{256,0},{384,128},{1,257},{129,385},{257,1},{385... | collective-permute-start | bytes 1769480 | tf_op jit(solution)/shard_map/ppermute | solution.py:312
  81.6 2.5 %collective-permute-start.5 = (bf16[1152,256]{1,0:T(8,128)(2,1)S(1)}, bf16[1152,256]{1,0:T(8,128)(2,1)S(1)}, u32[]{:S(2)}, u32[]{:S(2)}) collective-permute-start(bf16[1152,256]{1,0:T(8,128)(2,1)S(1)} %get-tuple-element.30), channel_id=1, source_target_pairs={{0,384},{128,0},{256,128},{384,256},{1,385},{129,1},{257,129},{385... | collective-permute-start | bytes 1769480 | tf_op jit(solution)/shard_map/ppermute | solution.py:312
  84.1 8.5 %collective-permute-done.3.r1 = bf16[1152,256]{1,0:T(8,128)(2,1)S(1)} collective-permute-done((bf16[1152,256]{1,0:T(8,128)(2,1)S(1)}, bf16[1152,256]{1,0:T(8,128)(2,1)S(1)}, u32[]{:S(2)}, u32[]{:S(2)}) %collective-permute-start.3) | collective-permute-done | bytes 589856 | tf_op jit(solution)/shard_map/ppermute | solution.py:312
  92.6 4.7 %collective-permute-done.4.r2 = bf16[1152,256]{1,0:T(8,128)(2,1)S(1)} collective-permute-done((bf16[1152,256]{1,0:T(8,128)(2,1)S(1)}, bf16[1152,256]{1,0:T(8,128)(2,1)S(1)}, u32[]{:S(2)}, u32[]{:S(2)}) %collective-permute-start.4) | collective-permute-done | bytes 589856 | tf_op jit(solution)/shard_map/ppermute | solution.py:312
  97.3 13.6 %collective-permute-done.5.r3 = bf16[1152,256]{1,0:T(8,128)(2,1)S(1)} collective-permute-done((bf16[1152,256]{1,0:T(8,128)(2,1)S(1)}, bf16[1152,256]{1,0:T(8,128)(2,1)S(1)}, u32[]{:S(2)}, u32[]{:S(2)}) %collective-permute-start.5) | collective-permute-done | bytes 589856 | tf_op jit(solution)/shard_map/ppermute | solution.py:312
  111.0 0.0 copy-start
  111.0 1.0 shard_map.121
  112.0 0.0 all-to-all-done.1
  112.0 0.0 copy-start.1
  112.0 0.0 copy-done
  112.0 0.6 copy-done.1
  112.6 1.4 %shard_map.120 = (bf16[128,1024]{1,0:T(8,128)(2,1)}, bf16[128,1024]{1,0:T(8,128)(2,1)}, f32[1,128]{1,0:T(1,128)}) custom-call(bf16[2048,256]{1,0:T(8,128)(2,1)S(1)} %bitcast.8, bf16[256,128]{1,0:T(8,128)(2,1)S(1)} %get-tuple-element.23.place, f32[1,128]{1,0:T(1,128)S(1)} %bitcast.11, bf16[128,1024]{1,0:T(8,128)(2,1)S(1)} %copy-done), custom_call_target="tpu_custom_call" | custom-call | flops 400000000 | bytes 2000000 | tf_op jit(solution)/shard_map/pallas_call | solution.py:286
Async XLA Ops:
  3.5 50.2 %all-to-all-start = ((bf16[128,16,256]{2,1,0:T(8,128)(2,1)}), bf16[128,16,256]{2,1,0:T(8,128)(2,1)S(1)}, u32[]{:S(2)}, u32[]{:S(2)}) async-start(bf16[128,16,256]{2,1,0:T(8,128)(2,1)} %bitcast.3), calls=%async_computation | async-start | bytes 2097152 | tf_op jit(solution)/shard_map/all_to_all | solution.py:316
  21.1 30.2 %collective-permute-start.2 = (bf16[1152,256]{1,0:T(8,128)(2,1)S(1)}, bf16[1152,256]{1,0:T(8,128)(2,1)S(1)}, u32[]{:S(2)}, u32[]{:S(2)}) collective-permute-start(bf16[1152,256]{1,0:T(8,128)(2,1)S(1)} %get-tuple-element.21), channel_id=1, source_target_pairs={{0,384},{128,0},{256,128},{384,256},{1,385},{129,1},{257,129},{385... | collective-permute-start | bytes 1769480 | tf_op jit(solution)/shard_map/ppermute | solution.py:312
  23.6 27.8 %collective-permute-start.1 = (bf16[1152,256]{1,0:T(8,128)(2,1)S(1)}, bf16[1152,256]{1,0:T(8,128)(2,1)S(1)}, u32[]{:S(2)}, u32[]{:S(2)}) collective-permute-start(bf16[1152,256]{1,0:T(8,128)(2,1)S(1)} %get-tuple-element.21), channel_id=1, source_target_pairs={{0,256},{128,384},{256,0},{384,128},{1,257},{129,385},{257,1},{385... | collective-permute-start | bytes 1769480 | tf_op jit(solution)/shard_map/ppermute | solution.py:312
  26.4 27.3 %collective-permute-start = (bf16[1152,256]{1,0:T(8,128)(2,1)S(1)}, bf16[1152,256]{1,0:T(8,128)(2,1)S(1)}, u32[]{:S(2)}, u32[]{:S(2)}) collective-permute-start(bf16[1152,256]{1,0:T(8,128)(2,1)S(1)} %get-tuple-element.21), channel_id=1, source_target_pairs={{0,128},{128,256},{256,384},{384,0},{1,129},{129,257},{257,385},{3... | collective-permute-start | bytes 1769480 | tf_op jit(solution)/shard_map/ppermute | solution.py:312
  51.4 2.3 %copy-start.2 = (bf16[1152,256]{1,0:T(8,128)(2,1)}, bf16[1152,256]{1,0:T(8,128)(2,1)S(1)}, u32[]{:S(2)}) copy-start(bf16[1152,256]{1,0:T(8,128)(2,1)S(1)} %collective-permute-done.2.w3) | copy-start | bytes 1769476
  51.4 2.3 %copy-start.3 = (bf16[1152,256]{1,0:T(8,128)(2,1)}, bf16[1152,256]{1,0:T(8,128)(2,1)S(1)}, u32[]{:S(2)}) copy-start(bf16[1152,256]{1,0:T(8,128)(2,1)S(1)} %collective-permute-done.1.w2) | copy-start | bytes 1769476
  53.6 0.8 copy-start.4
  60.5 51.4 %all-to-all-start.1 = ((bf16[128,16,256]{2,1,0:T(8,128)(2,1)}), bf16[128,16,256]{2,1,0:T(8,128)(2,1)S(1)}, u32[]{:S(2)}, u32[]{:S(2)}) async-start(bf16[128,16,256]{2,1,0:T(8,128)(2,1)} %bitcast.5), calls=%async_computation.1 | async-start | bytes 2097152 | tf_op jit(solution)/shard_map/all_to_all | solution.py:316
  75.4 17.2 %collective-permute-start.3 = (bf16[1152,256]{1,0:T(8,128)(2,1)S(1)}, bf16[1152,256]{1,0:T(8,128)(2,1)S(1)}, u32[]{:S(2)}, u32[]{:S(2)}) collective-permute-start(bf16[1152,256]{1,0:T(8,128)(2,1)S(1)} %get-tuple-element.28), channel_id=1, source_target_pairs={{0,128},{128,256},{256,384},{384,0},{1,129},{129,257},{257,385},{3... | collective-permute-start | bytes 1769480 | tf_op jit(solution)/shard_map/ppermute | solution.py:312
  79.7 17.7 %collective-permute-start.4 = (bf16[1152,256]{1,0:T(8,128)(2,1)S(1)}, bf16[1152,256]{1,0:T(8,128)(2,1)S(1)}, u32[]{:S(2)}, u32[]{:S(2)}) collective-permute-start(bf16[1152,256]{1,0:T(8,128)(2,1)S(1)} %get-tuple-element.29), channel_id=1, source_target_pairs={{0,256},{128,384},{256,0},{384,128},{1,257},{129,385},{257,1},{385... | collective-permute-start | bytes 1769480 | tf_op jit(solution)/shard_map/ppermute | solution.py:312
  81.6 29.4 %collective-permute-start.5 = (bf16[1152,256]{1,0:T(8,128)(2,1)S(1)}, bf16[1152,256]{1,0:T(8,128)(2,1)S(1)}, u32[]{:S(2)}, u32[]{:S(2)}) collective-permute-start(bf16[1152,256]{1,0:T(8,128)(2,1)S(1)} %get-tuple-element.30), channel_id=1, source_target_pairs={{0,384},{128,0},{256,128},{384,256},{1,385},{129,1},{257,129},{385... | collective-permute-start | bytes 1769480 | tf_op jit(solution)/shard_map/ppermute | solution.py:312
  111.0 1.0 copy-start
  112.0 0.7 copy-start.1

commit v3 on v2

--- a/solution.py
+++ b/solution.py
@@ -109,35 +109,37 @@
 
 
 def expert_kernel(
-    index, recv, wg, wu, wd, w1, w2, w3, send, g0, g1, g2, g3,
-    rows, outs, shards, send_v, grads_v, own_sems, in_sems, out_sems, grad_sems,
+    index, recv, wg, wu, wd, w1, w2, w3, send, g2, rows_out, slopes_out, hidden_out,
+    outs, w0, send_v, g2_v, rows, slopes, hidden_v, own_sems, out_sems,
 ):
     me = index[0]
-    arriving = [weight_copies(wg, wu, wd, shards.at[0], own_sems)]
-    for k, w in enumerate((w1, w2, w3)):
-        arriving.append((pltpu.make_async_copy(w, shards.at[k + 1], in_sems.at[k]),))
-    for copies in arriving:
-        for copy in copies:
-            copy.start()
+    arriving = weight_copies(wg, wu, wd, w0, own_sems)
+    for copy in arriving:
+        copy.start()
     sort = sorting()
     for b in range(8):
         block = mm(sort, recv[b * 256 : b * 256 + 256, :]).astype(BF)
         for piece in range(8):
             rows[piece, b * 32 : b * 32 + 32, :] = block[piece * 32 : piece * 32 + 32, :]
     gate_lo = up_lo = both_hi = backed = None
-    for k in range(4):
-        for copy in arriving[k]:
-            copy.wait()
+    leaving = [pltpu.make_async_copy(rows, rows_out, out_sems.at[8])]
+    leaving[0].start()
+    shards = (w0, w1, w2, w3)
+    for k in (1, 2, 3, 0):
+        if k == 0:
+            for copy in arriving:
+                copy.wait()
+        w = shards[k]
         q = (me + 4 - k) & 3
         xq = rows[q]
         sq = rows[4 + q]
         terms = (
-            mm(xq, shards[k, 0:256, :]),
-            mm(xq, shards[k, 256:512, :]),
-            mm(xq, shards[k, 512:768, :]),
-            mm_nt(sq, shards[k, 768:1152, :]),
+            mm(xq, w[0:256, :]),
+            mm(xq, w[256:512, :]),
+            mm(xq, w[512:768, :]),
+            mm_nt(sq, w[768:1152, :]),
         )
-        if k == 0:
+        if k == 1:
             gate_lo, up_lo, both_hi, backed = terms
         else:
             gate_lo, up_lo, both_hi, backed = (
@@ -155,37 +157,56 @@
     dg_lo = d_gate[:, 0:256]
     du_lo = d_up[:, 0:256]
     d_hi = jnp.concatenate([d_gate[:, 256:384], d_up[:, 256:384]], 1)
+    hidden_v[...] = hidden
+    slopes[0] = dg_lo
+    slopes[1] = du_lo
+    slopes[2] = d_hi
+    grads_of((me + 2) & 3, g2_v, rows, slopes, hidden_v)
+    for n, (source, target) in enumerate(
+        ((hidden_v, hidden_out), (slopes, slopes_out), (g2_v, g2))
+    ):
+        leaving.append(pltpu.make_async_copy(source, target, out_sems.at[9 + n]))
+        leaving[-1].start()
     for k in range(4):
         q = (me + 4 - k) & 3
-        outs[q] = mm(hidden, shards[k, 768:1152, :]).astype(BF)
+        w = shards[k]
+        outs[q] = mm(hidden, w[768:1152, :]).astype(BF)
         outs[4 + q] = (
-            mm_nt(dg_lo, shards[k, 0:256, :])
-            + mm_nt(du_lo, shards[k, 256:512, :])
-            + mm_nt(d_hi, shards[k, 512:768, :])
+            mm_nt(dg_lo, w[0:256, :]) + mm_nt(du_lo, w[256:512, :]) + mm_nt(d_hi, w[512:768, :])
         ).astype(BF)
     back = unsorting()
-    leaving = []
     for b in range(8):
         block = jnp.concatenate([outs[p, b * 32 : b * 32 + 32, :] for p in range(8)], 0)
         part = pl.ds(b * 256, 256)
         send_v[part, :] = mm(back, block).astype(BF)
         leaving.append(pltpu.make_async_copy(send_v.at[part, :], send.at[part, :], out_sems.at[b]))
         leaving[-1].start()
-    for k, g in ((2, g2), (1, g1), (3, g3), (0, g0)):
-        q = (me + k) & 3
-        xq = rows[q]
-        sq = rows[4 + q]
-        grads_v[k, 0:256, :] = mm_tn(xq, dg_lo).astype(BF)
-        grads_v[k, 256:512, :] = mm_tn(xq, du_lo).astype(BF)
-        grads_v[k, 512:768, :] = mm_tn(xq, d_hi).astype(BF)
-        grads_v[k, 768:1152, :] = mm_tn(hidden, sq).astype(BF)
-        leaving.append(pltpu.make_async_copy(grads_v.at[k], g, grad_sems.at[k]))
-        leaving[-1].start()
     for copy in leaving:
         copy.wait()
 
 
-def unpack_kernel(recv, place, gates, cot, gated_out, input_grad, gate_grad, flat):
+def grads_of(q, out, rows, slopes, hidden):
+    for part in range(3):
+        out[part * 256 : part * 256 + 256, :] = mm_tn(rows[q], slopes[part]).astype(BF)
+    out[768:1152, :] = mm_tn(hidden[...], rows[4 + q]).astype(BF)
+
+
+def grads_kernel(index, rows, slopes, hidden, g1, g3, g0):
+    me = index[0]
+    for k, g in ((1, g1), (3, g3), (0, g0)):
+        grads_of((me + k) & 3, g, rows, slopes, hidden)
+
+
+def unpack_kernel(
+    recv, place, gates_hbm, cot_hbm, gated_out, input_grad, gate_grad,
+    flat, gates, cot, gated_v, input_v, in_sems, out_sems,
+):
+    arriving = (
+        pltpu.make_async_copy(gates_hbm, gates, in_sems.at[0]),
+        pltpu.make_async_copy(cot_hbm, cot, in_sems.at[1]),
+    )
+    for copy in arriving:
+        copy.start()
     sort = sorting()
     for b in range(8):
         block = mm(sort, recv[b * 256 : b * 256 + 256, :]).astype(BF)
@@ -194,16 +215,24 @@
                 piece * 32 : piece * 32 + 32, :
             ]
     onehot = place[...]
+    input_v[...] = mm_tn(onehot, flat[:, 1024:2048]).astype(BF)
+    leaving = [pltpu.make_async_copy(input_v, input_grad, out_sems.at[0])]
+    leaving[0].start()
+    row_out = mm_tn(onehot, flat[:, 0:1024])
+    for copy in arriving:
+        copy.wait()
     gate = columns_of(gates[...])
     total = jnp.zeros((128, 128), F32)
-    row_out = mm_tn(onehot, flat[:, 0:1024])
     for part in range(8):
         cols = slice(part * 128, part * 128 + 128)
         piece = row_out[:, cols]
-        gated_out[:, cols] = (gate * piece).astype(BF)
+        gated_v[:, cols] = (gate * piece).astype(BF)
         total = total + cot[:, cols].astype(F32) * piece
+    leaving.append(pltpu.make_async_copy(gated_v, gated_out, out_sems.at[1]))
+    leaving[1].start()
     gate_grad[...] = jnp.sum(jnp.transpose(total), axis=0, keepdims=True)
-    input_grad[...] = mm_tn(onehot, flat[:, 1024:2048]).astype(BF)
+    for copy in leaving:
+        copy.wait()
 
 
 def sum_kernel(g0, r1, r2, r3, out_gate, out_up, out_down):
@@ -226,7 +255,9 @@
 def call(kernel, outs, specs, out_specs, flops, moved, scratch=(), limit=12 << 20):
     return pl.pallas_call(
         kernel,
-        out_shape=[jax.ShapeDtypeStruct(s, d) for s, d in outs],
+        out_shape=[
+            pltpu.HBM(o[0], o[1]) if len(o) == 3 else jax.ShapeDtypeStruct(*o) for o in outs
+        ],
         in_specs=specs,
         out_specs=out_specs,
         scratch_shapes=list(scratch),
@@ -262,36 +293,56 @@
 def expert_rows(index, recv, wg, wu, wd, shards):
     return call(
         expert_kernel,
-        [((2048, 256), BF)] + [((1152, 256), BF)] * 4,
-        [SMEM, VMEM] + [HBM] * 6,
+        [
+            ((2048, 256), BF),
+            ((1152, 256), BF, True),
+            ((8, 256, 256), BF, True),
+            ((3, 256, 256), BF, True),
+            ((256, 384), BF, True),
+        ],
+        [SMEM, VMEM] + [HBM] * 3 + [VMEM] * 3,
         [HBM] * 5,
-        2400000000,
-        7000000,
+        2000000000,
+        6000000,
         [
             pltpu.VMEM((8, 256, 256), BF),
+            pltpu.VMEM((1152, 256), BF),
+            pltpu.VMEM((2048, 256), BF),
+            pltpu.VMEM((1152, 256), BF),
             pltpu.VMEM((8, 256, 256), BF),
-            pltpu.VMEM((4, 1152, 256), BF),
-            pltpu.VMEM((2048, 256), BF),
-            pltpu.VMEM((4, 1152, 256), BF),
+            pltpu.VMEM((3, 256, 256), BF),
+            pltpu.VMEM((256, 384), BF),
             pltpu.SemaphoreType.DMA((5,)),
-            pltpu.SemaphoreType.DMA((3,)),
-            pltpu.SemaphoreType.DMA((8,)),
-            pltpu.SemaphoreType.DMA((4,)),
+            pltpu.SemaphoreType.DMA((12,)),
         ],
         24 << 20,
-    )(index, recv, *map(hbm, (wg, wu, wd, *shards)))
+    )(index, recv, *map(hbm, (wg, wu, wd)), *shards)
+
+
+def other_grads(index, rows, slopes, hidden):
+    return call(
+        grads_kernel, [((1152, 256), BF)] * 3, [SMEM] + [VMEM] * 3, [VMEM] * 3, 450000000, 3000000
+    )(index, rows, slopes, hidden)
 
 
 def unpack_rows(recv, place, gates, cot):
     return call(
         unpack_kernel,
         [((128, 1024), BF), ((128, 1024), BF), ((1, 128), F32)],
-        [VMEM] * 4,
-        [VMEM] * 3,
+        [VMEM, VMEM, HBM, HBM],
+        [HBM, HBM, VMEM],
         400000000,
         2000000,
-        [pltpu.VMEM((256, 2048), BF)],
-    )(recv, place, gates, cot)
+        [
+            pltpu.VMEM((256, 2048), BF),
+            pltpu.VMEM((1, 128), F32),
+            pltpu.VMEM((128, 1024), BF),
+            pltpu.VMEM((128, 1024), BF),
+            pltpu.VMEM((128, 1024), BF),
+            pltpu.SemaphoreType.DMA((2,)),
+            pltpu.SemaphoreType.DMA((2,)),
+        ],
+    )(recv, place, hbm(gates), hbm(cot))
 
 
 def sum_grads(parts):
@@ -324,11 +375,13 @@
         shards.append(shift(own, k))
     recv = exchange(send)
     index = lax.axis_index("dp").astype(jnp.int32).reshape(1)
-    out = expert_rows(index, recv, w_gate, w_up, w_down, shards)
-    returned = exchange(out[0])
-    parts = [out[1]]
-    for k in (1, 2, 3):
-        parts.append(shift(out[1 + k], k))
+    out, g2, rows, slopes, hidden = expert_rows(index, recv, w_gate, w_up, w_down, shards)
+    returned = exchange(out)
+    r2 = shift(g2, 2)
+    g1, g3, g0 = other_grads(index, rows, slopes, hidden)
+    r1 = shift(g1, 1)
+    r3 = shift(g3, 3)
+    parts = (g0, r1, r2, r3)
     gated_out, input_grad, gate_grad = unpack_rows(returned, place, gate_row, cotangent)
     grads = sum_grads(parts)
     return (gated_out, input_grad, gate_grad.reshape(128, 1), *grads)

time: 115 us -> 112 us (0.974)
  the two profiles are of different devices: /device:TPU:15 before, /device:TPU:1 now
where the time goes in v3:
time: 112 us
  starting transfers between devices  50.6 us (45%)
  waiting for transfers between devices  48.2 us (43%)
  Pallas kernels  12.1 us (11%)
    ppermute x6, waiting for transfers between devices, shift(): lax.ppermute(value, 'dp', [(i, (i + k) % groups) for i in range(groups)])  48.2 us
    all_to_all x2, starting transfers between devices, exchange(): lax.all_to_all(wire, 'expert', split_axis=0, concat_axis=0, tiled=True)  32.4 us
    ppermute x6, starting transfers between devices, shift(): lax.ppermute(value, 'dp', [(i, (i + k) % groups) for i in range(groups)])  18.2 us
    pallas_call x1, Pallas kernels, expert_rows(): call(expert_kernel, [((2048, 256), BF), ((1152, 256), BF, True), ((8, 256...  4.98 us
    pallas_call x1, Pallas kernels, pack(): call(pack_kernel, [((1152, 256), BF), ((2048, 256), BF), ((256, 128), BF)...  2.85 us
    pallas_call x1, Pallas kernels, unpack_rows(): call(unpack_kernel, [((128, 1024), BF), ((128, 1024), BF), ((1, 128), F32...  2.64 us
  transfers between devices with their start and end apart: 8, of which 5 were waited for; matrix products, arithmetic and copies ran while one was open for 0% of the time, Pallas kernels for 1%

profile of v3, /device:TPU:1, one launch (start us, length us, event | category | flops | bytes accessed | tf_op | source)
XLA Modules:
  0.0 111.7 jit_solution(10803355019539675768)
XLA Ops:
  0.6 2.8 %shard_map.118 = (bf16[1152,256]{1,0:T(8,128)(2,1)S(1)}, bf16[2048,256]{1,0:T(8,128)(2,1)}, bf16[256,128]{1,0:T(8,128)(2,1)S(1)}) custom-call(s32[1,128]{1,0:T(1,128)} %bitcast.10, f32[1,128]{1,0:T(1,128)} %bitcast.11, bf16[128,1024]{1,0:T(8,128)(2,1)} %x.1, bf16[128,1024]{1,0:T(8,128)(2,1)} %cot_hbm.1, bf16[1,256,384]{2,1,0:T(8,128)(2,1)} %wg.3, ...), custom_call_target="tpu_custom_call" | custom-call | flops 400000000 | bytes 2600000 | tf_op jit(solution)/shard_map/pallas_call | solution.py:274
  3.5 18.4 %all-to-all-start = ((bf16[128,16,256]{2,1,0:T(8,128)(2,1)}), bf16[128,16,256]{2,1,0:T(8,128)(2,1)S(1)}, u32[]{:S(2)}, u32[]{:S(2)}) async-start(bf16[128,16,256]{2,1,0:T(8,128)(2,1)} %bitcast.3), calls=%async_computation | async-start | bytes 2097152 | tf_op jit(solution)/shard_map/all_to_all | solution.py:367
  21.9 4.4 %collective-permute-start.2 = (bf16[1152,256]{1,0:T(8,128)(2,1)S(1)}, bf16[1152,256]{1,0:T(8,128)(2,1)S(1)}, u32[]{:S(2)}, u32[]{:S(2)}) collective-permute-start(bf16[1152,256]{1,0:T(8,128)(2,1)S(1)} %get-tuple-element.24), channel_id=1, source_target_pairs={{0,384},{128,0},{256,128},{384,256},{1,385},{129,1},{257,129},{385... | collective-permute-start | bytes 1769480 | tf_op jit(solution)/shard_map/ppermute | solution.py:363
  26.3 2.4 %collective-permute-start.1 = (bf16[1152,256]{1,0:T(8,128)(2,1)S(1)}, bf16[1152,256]{1,0:T(8,128)(2,1)S(1)}, u32[]{:S(2)}, u32[]{:S(2)}) collective-permute-start(bf16[1152,256]{1,0:T(8,128)(2,1)S(1)} %get-tuple-element.24), channel_id=1, source_target_pairs={{0,256},{128,384},{256,0},{384,128},{1,257},{129,385},{257,1},{385... | collective-permute-start | bytes 1769480 | tf_op jit(solution)/shard_map/ppermute | solution.py:363
  28.7 2.5 %collective-permute-start = (bf16[1152,256]{1,0:T(8,128)(2,1)S(1)}, bf16[1152,256]{1,0:T(8,128)(2,1)S(1)}, u32[]{:S(2)}, u32[]{:S(2)}) collective-permute-start(bf16[1152,256]{1,0:T(8,128)(2,1)S(1)} %get-tuple-element.24), channel_id=1, source_target_pairs={{0,128},{128,256},{256,384},{384,0},{1,129},{129,257},{257,385},{3... | collective-permute-start | bytes 1769480 | tf_op jit(solution)/shard_map/ppermute | solution.py:363
  31.3 7.6 %collective-permute-done.2.w3 = bf16[1152,256]{1,0:T(8,128)(2,1)S(1)} collective-permute-done((bf16[1152,256]{1,0:T(8,128)(2,1)S(1)}, bf16[1152,256]{1,0:T(8,128)(2,1)S(1)}, u32[]{:S(2)}, u32[]{:S(2)}) %collective-permute-start.2) | collective-permute-done | bytes 589856 | tf_op jit(solution)/shard_map/ppermute | solution.py:363
  38.9 4.6 %collective-permute-done.1.w2 = bf16[1152,256]{1,0:T(8,128)(2,1)S(1)} collective-permute-done((bf16[1152,256]{1,0:T(8,128)(2,1)S(1)}, bf16[1152,256]{1,0:T(8,128)(2,1)S(1)}, u32[]{:S(2)}, u32[]{:S(2)}) %collective-permute-start.1) | collective-permute-done | bytes 589856 | tf_op jit(solution)/shard_map/ppermute | solution.py:363
  43.5 14.1 %collective-permute-done.w1 = bf16[1152,256]{1,0:T(8,128)(2,1)S(1)} collective-permute-done((bf16[1152,256]{1,0:T(8,128)(2,1)S(1)}, bf16[1152,256]{1,0:T(8,128)(2,1)S(1)}, u32[]{:S(2)}, u32[]{:S(2)}) %collective-permute-start) | collective-permute-done | bytes 589856 | tf_op jit(solution)/shard_map/ppermute | solution.py:363
  57.6 0.0 all-to-all-done
  57.6 5.0 %shard_map.119 = (bf16[2048,256]{1,0:T(8,128)(2,1)}, bf16[1152,256]{1,0:T(8,128)(2,1)}, bf16[8,256,256]{2,1,0:T(8,128)(2,1)}, bf16[3,256,256]{2,1,0:T(8,128)(2,1)}, bf16[256,384]{1,0:T(8,128)(2,1)}) custom-call(s32[1]{0:T(128)} %bitcast.index, bf16[2048,256]{1,0:T(8,128)(2,1)S(1)} %bitcast.9, bf16[1,256,384]{2,1,0:T(8,128)(2,1)} %wg.3, ...), custom_call_target="tpu_custom_call" | custom-call | flops 2000000000 | bytes 6000000 | tf_op jit(solution)/shard_map/pallas_call | solution.py:294
  62.6 0.0 copy-start
  62.6 0.0 copy-start.1
  62.6 0.0 copy-start.2
  62.6 14.0 %all-to-all-start.1 = ((bf16[128,16,256]{2,1,0:T(8,128)(2,1)}), bf16[128,16,256]{2,1,0:T(8,128)(2,1)S(1)}, u32[]{:S(2)}, u32[]{:S(2)}) async-start(bf16[128,16,256]{2,1,0:T(8,128)(2,1)} %bitcast.5), calls=%async_computation.1 | async-start | bytes 2097152 | tf_op jit(solution)/shard_map/all_to_all | solution.py:367
  76.6 2.4 %collective-permute-start.4 = (bf16[1152,256]{1,0:T(8,128)(2,1)}, bf16[1152,256]{1,0:T(8,128)(2,1)S(1)}, u32[]{:S(2)}, u32[]{:S(2)}) collective-permute-start(bf16[1152,256]{1,0:T(8,128)(2,1)} %get-tuple-element.35), channel_id=1, source_target_pairs={{0,256},{128,384},{256,0},{384,128},{1,257},{129,385},{257,1},{385... | collective-permute-start | bytes 1769480 | tf_op jit(solution)/shard_map/ppermute | solution.py:363
  79.0 0.0 copy-done
  79.1 0.0 copy-done.1
  79.1 0.0 copy-done.2
  79.1 0.7 shard_map.121
  79.8 2.3 %collective-permute-start.3 = (bf16[1152,256]{1,0:T(8,128)(2,1)S(1)}, bf16[1152,256]{1,0:T(8,128)(2,1)S(1)}, u32[]{:S(2)}, u32[]{:S(2)}) collective-permute-start(bf16[1152,256]{1,0:T(8,128)(2,1)S(1)} %get-tuple-element.34), channel_id=1, source_target_pairs={{0,128},{128,256},{256,384},{384,0},{1,129},{129,257},{257,385},{3... | collective-permute-start | bytes 1769480 | tf_op jit(solution)/shard_map/ppermute | solution.py:363
  82.1 4.2 %collective-permute-start.5 = (bf16[1152,256]{1,0:T(8,128)(2,1)S(1)}, bf16[1152,256]{1,0:T(8,128)(2,1)S(1)}, u32[]{:S(2)}, u32[]{:S(2)}) collective-permute-start(bf16[1152,256]{1,0:T(8,128)(2,1)S(1)} %get-tuple-element.36), channel_id=1, source_target_pairs={{0,384},{128,0},{256,128},{384,256},{1,385},{129,1},{257,129},{385... | collective-permute-start | bytes 1769480 | tf_op jit(solution)/shard_map/ppermute | solution.py:363
  86.3 8.0 %collective-permute-done.4.r2 = bf16[1152,256]{1,0:T(8,128)(2,1)S(1)} collective-permute-done((bf16[1152,256]{1,0:T(8,128)(2,1)}, bf16[1152,256]{1,0:T(8,128)(2,1)S(1)}, u32[]{:S(2)}, u32[]{:S(2)}) %collective-permute-start.4) | collective-permute-done | bytes 589856 | tf_op jit(solution)/shard_map/ppermute | solution.py:363
  94.2 13.9 %collective-permute-done.3.r1 = bf16[1152,256]{1,0:T(8,128)(2,1)S(1)} collective-permute-done((bf16[1152,256]{1,0:T(8,128)(2,1)S(1)}, bf16[1152,256]{1,0:T(8,128)(2,1)S(1)}, u32[]{:S(2)}, u32[]{:S(2)}) %collective-permute-start.3) | collective-permute-done | bytes 589856 | tf_op jit(solution)/shard_map/ppermute | solution.py:363
  108.1 0.0 collective-permute-done.5.r3
  108.1 1.0 shard_map.122
  109.1 0.0 all-to-all-done.1
  109.1 2.6 %shard_map.120 = (bf16[128,1024]{1,0:T(8,128)(2,1)}, bf16[128,1024]{1,0:T(8,128)(2,1)}, f32[1,128]{1,0:T(1,128)}) custom-call(bf16[2048,256]{1,0:T(8,128)(2,1)S(1)} %bitcast.8, bf16[256,128]{1,0:T(8,128)(2,1)S(1)} %get-tuple-element.26.place, f32[1,128]{1,0:T(1,128)} %bitcast.12, bf16[128,1024]{1,0:T(8,128)(2,1)} %cot_hbm.1), custom_call_target="tpu_custom_call" | custom-call | flops 400000000 | bytes 2000000 | tf_op jit(solution)/shard_map/pallas_call | solution.py:329
Async XLA Ops:
  3.5 54.1 %all-to-all-start = ((bf16[128,16,256]{2,1,0:T(8,128)(2,1)}), bf16[128,16,256]{2,1,0:T(8,128)(2,1)S(1)}, u32[]{:S(2)}, u32[]{:S(2)}) async-start(bf16[128,16,256]{2,1,0:T(8,128)(2,1)} %bitcast.3), calls=%async_computation | async-start | bytes 2097152 | tf_op jit(solution)/shard_map/all_to_all | solution.py:367
  21.9 17.0 %collective-permute-start.2 = (bf16[1152,256]{1,0:T(8,128)(2,1)S(1)}, bf16[1152,256]{1,0:T(8,128)(2,1)S(1)}, u32[]{:S(2)}, u32[]{:S(2)}) collective-permute-start(bf16[1152,256]{1,0:T(8,128)(2,1)S(1)} %get-tuple-element.24), channel_id=1, source_target_pairs={{0,384},{128,0},{256,128},{384,256},{1,385},{129,1},{257,129},{385... | collective-permute-start | bytes 1769480 | tf_op jit(solution)/shard_map/ppermute | solution.py:363
  26.3 17.2 %collective-permute-start.1 = (bf16[1152,256]{1,0:T(8,128)(2,1)S(1)}, bf16[1152,256]{1,0:T(8,128)(2,1)S(1)}, u32[]{:S(2)}, u32[]{:S(2)}) collective-permute-start(bf16[1152,256]{1,0:T(8,128)(2,1)S(1)} %get-tuple-element.24), channel_id=1, source_target_pairs={{0,256},{128,384},{256,0},{384,128},{1,257},{129,385},{257,1},{385... | collective-permute-start | bytes 1769480 | tf_op jit(solution)/shard_map/ppermute | solution.py:363
  28.7 28.8 %collective-permute-start = (bf16[1152,256]{1,0:T(8,128)(2,1)S(1)}, bf16[1152,256]{1,0:T(8,128)(2,1)S(1)}, u32[]{:S(2)}, u32[]{:S(2)}) collective-permute-start(bf16[1152,256]{1,0:T(8,128)(2,1)S(1)} %get-tuple-element.24), channel_id=1, source_target_pairs={{0,128},{128,256},{256,384},{384,0},{1,129},{129,257},{257,385},{3... | collective-permute-start | bytes 1769480 | tf_op jit(solution)/shard_map/ppermute | solution.py:363
  62.6 16.5 %copy-start = (bf16[8,256,256]{2,1,0:T(8,128)(2,1)S(1)}, bf16[8,256,256]{2,1,0:T(8,128)(2,1)}, u32[]{:S(2)}) copy-start(bf16[8,256,256]{2,1,0:T(8,128)(2,1)} %get-tuple-element.30.rows) | copy-start | bytes 3145732
  62.6 16.5 %copy-start.1 = (bf16[3,256,256]{2,1,0:T(8,128)(2,1)S(1)}, bf16[3,256,256]{2,1,0:T(8,128)(2,1)}, u32[]{:S(2)}) copy-start(bf16[3,256,256]{2,1,0:T(8,128)(2,1)} %get-tuple-element.31.slopes) | copy-start | bytes 1179652
  62.6 16.5 %copy-start.2 = (bf16[256,384]{1,0:T(8,128)(2,1)S(1)}, bf16[256,384]{1,0:T(8,128)(2,1)}, u32[]{:S(2)}) copy-start(bf16[256,384]{1,0:T(8,128)(2,1)} %get-tuple-element.32.hidden) | copy-start | bytes 589828
  62.6 46.5 %all-to-all-start.1 = ((bf16[128,16,256]{2,1,0:T(8,128)(2,1)}), bf16[128,16,256]{2,1,0:T(8,128)(2,1)S(1)}, u32[]{:S(2)}, u32[]{:S(2)}) async-start(bf16[128,16,256]{2,1,0:T(8,128)(2,1)} %bitcast.5), calls=%async_computation.1 | async-start | bytes 2097152 | tf_op jit(solution)/shard_map/all_to_all | solution.py:367
  76.6 17.6 %collective-permute-start.4 = (bf16[1152,256]{1,0:T(8,128)(2,1)}, bf16[1152,256]{1,0:T(8,128)(2,1)S(1)}, u32[]{:S(2)}, u32[]{:S(2)}) collective-permute-start(bf16[1152,256]{1,0:T(8,128)(2,1)} %get-tuple-element.35), channel_id=1, source_target_pairs={{0,256},{128,384},{256,0},{384,128},{1,257},{129,385},{257,1},{385... | collective-permute-start | bytes 1769480 | tf_op jit(solution)/shard_map/ppermute | solution.py:363
  79.8 28.3 %collective-permute-start.3 = (bf16[1152,256]{1,0:T(8,128)(2,1)S(1)}, bf16[1152,256]{1,0:T(8,128)(2,1)S(1)}, u32[]{:S(2)}, u32[]{:S(2)}) collective-permute-start(bf16[1152,256]{1,0:T(8,128)(2,1)S(1)} %get-tuple-element.34), channel_id=1, source_target_pairs={{0,128},{128,256},{256,384},{384,0},{1,129},{129,257},{257,385},{3... | collective-permute-start | bytes 1769480 | tf_op jit(solution)/shard_map/ppermute | solution.py:363
  82.1 26.0 %collective-permute-start.5 = (bf16[1152,256]{1,0:T(8,128)(2,1)S(1)}, bf16[1152,256]{1,0:T(8,128)(2,1)S(1)}, u32[]{:S(2)}, u32[]{:S(2)}) collective-permute-start(bf16[1152,256]{1,0:T(8,128)(2,1)S(1)} %get-tuple-element.36), channel_id=1, source_target_pairs={{0,384},{128,0},{256,128},{384,256},{1,385},{129,1},{257,129},{385... | collective-permute-start | bytes 1769480 | tf_op jit(solution)/shard_map/ppermute | solution.py:363

commit v4 on v3

--- a/solution.py
+++ b/solution.py
@@ -56,7 +56,7 @@
 
 
 def pack_kernel(
-    ids, gates, x, cot, wg, wu, wd, own, send, place, ids_v, gates_v, x_v, cot_v, send_v, sems, out_sems
+    ids, gates, x, cot, wg, wu, wd, own, send, place, gates_v, ids_v, x_v, cot_v, send_v, sems, out_sems
 ):
     small = (
         pltpu.make_async_copy(ids, ids_v, sems.at[5]),
@@ -109,13 +109,10 @@
 
 
 def expert_kernel(
-    index, recv, wg, wu, wd, w1, w2, w3, send, g2, rows_out, slopes_out, hidden_out,
-    outs, w0, send_v, g2_v, rows, slopes, hidden_v, own_sems, out_sems,
+    index, recv, w0, w1, w2, w3, send, g2, rows_out, slopes_out, hidden_out,
+    outs, send_v, g2_v, rows, slopes, hidden_v, out_sems,
 ):
     me = index[0]
-    arriving = weight_copies(wg, wu, wd, w0, own_sems)
-    for copy in arriving:
-        copy.start()
     sort = sorting()
     for b in range(8):
         block = mm(sort, recv[b * 256 : b * 256 + 256, :]).astype(BF)
@@ -125,10 +122,7 @@
     leaving = [pltpu.make_async_copy(rows, rows_out, out_sems.at[8])]
     leaving[0].start()
     shards = (w0, w1, w2, w3)
-    for k in (1, 2, 3, 0):
-        if k == 0:
-            for copy in arriving:
-                copy.wait()
+    for k in range(4):
         w = shards[k]
         q = (me + 4 - k) & 3
         xq = rows[q]
@@ -139,7 +133,7 @@
             mm(xq, w[512:768, :]),
             mm_nt(sq, w[768:1152, :]),
         )
-        if k == 1:
+        if k == 0:
             gate_lo, up_lo, both_hi, backed = terms
         else:
             gate_lo, up_lo, both_hi, backed = (
@@ -197,16 +191,7 @@
         grads_of((me + k) & 3, g, rows, slopes, hidden)
 
 
-def unpack_kernel(
-    recv, place, gates_hbm, cot_hbm, gated_out, input_grad, gate_grad,
-    flat, gates, cot, gated_v, input_v, in_sems, out_sems,
-):
-    arriving = (
-        pltpu.make_async_copy(gates_hbm, gates, in_sems.at[0]),
-        pltpu.make_async_copy(cot_hbm, cot, in_sems.at[1]),
-    )
-    for copy in arriving:
-        copy.start()
+def unpack_kernel(recv, place, gates, cot, gated_out, input_grad, gate_grad, flat):
     sort = sorting()
     for b in range(8):
         block = mm(sort, recv[b * 256 : b * 256 + 256, :]).astype(BF)
@@ -215,24 +200,16 @@
                 piece * 32 : piece * 32 + 32, :
             ]
     onehot = place[...]
-    input_v[...] = mm_tn(onehot, flat[:, 1024:2048]).astype(BF)
-    leaving = [pltpu.make_async_copy(input_v, input_grad, out_sems.at[0])]
-    leaving[0].start()
-    row_out = mm_tn(onehot, flat[:, 0:1024])
-    for copy in arriving:
-        copy.wait()
     gate = columns_of(gates[...])
     total = jnp.zeros((128, 128), F32)
+    row_out = mm_tn(onehot, flat[:, 0:1024])
     for part in range(8):
         cols = slice(part * 128, part * 128 + 128)
         piece = row_out[:, cols]
-        gated_v[:, cols] = (gate * piece).astype(BF)
+        gated_out[:, cols] = (gate * piece).astype(BF)
         total = total + cot[:, cols].astype(F32) * piece
-    leaving.append(pltpu.make_async_copy(gated_v, gated_out, out_sems.at[1]))
-    leaving[1].start()
     gate_grad[...] = jnp.sum(jnp.transpose(total), axis=0, keepdims=True)
-    for copy in leaving:
-        copy.wait()
+    input_grad[...] = mm_tn(onehot, flat[:, 1024:2048]).astype(BF)
 
 
 def sum_kernel(g0, r1, r2, r3, out_gate, out_up, out_down):
@@ -273,14 +250,13 @@
 def pack(ids, gates, x, cot, wg, wu, wd):
     return call(
         pack_kernel,
-        [((1152, 256), BF), ((2048, 256), BF), ((256, 128), BF)],
+        [((1152, 256), BF), ((2048, 256), BF), ((256, 128), BF), ((1, 128), F32)],
         [HBM] * 7,
-        [VMEM, HBM, VMEM],
+        [VMEM, HBM, VMEM, VMEM],
         400000000,
         2600000,
         [
             pltpu.VMEM((1, 128), jnp.int32),
-            pltpu.VMEM((1, 128), F32),
             pltpu.VMEM((128, 1024), BF),
             pltpu.VMEM((128, 1024), BF),
             pltpu.VMEM((2048, 256), BF),
@@ -290,7 +266,7 @@
     )(*map(hbm, (ids, gates, x, cot, wg, wu, wd)))
 
 
-def expert_rows(index, recv, wg, wu, wd, shards):
+def expert_rows(index, recv, shards):
     return call(
         expert_kernel,
         [
@@ -300,23 +276,21 @@
             ((3, 256, 256), BF, True),
             ((256, 384), BF, True),
         ],
-        [SMEM, VMEM] + [HBM] * 3 + [VMEM] * 3,
+        [SMEM] + [VMEM] * 5,
         [HBM] * 5,
         2000000000,
         6000000,
         [
             pltpu.VMEM((8, 256, 256), BF),
-            pltpu.VMEM((1152, 256), BF),
             pltpu.VMEM((2048, 256), BF),
             pltpu.VMEM((1152, 256), BF),
             pltpu.VMEM((8, 256, 256), BF),
             pltpu.VMEM((3, 256, 256), BF),
             pltpu.VMEM((256, 384), BF),
-            pltpu.SemaphoreType.DMA((5,)),
             pltpu.SemaphoreType.DMA((12,)),
         ],
         24 << 20,
-    )(index, recv, *map(hbm, (wg, wu, wd)), *shards)
+    )(index, recv, *shards)
 
 
 def other_grads(index, rows, slopes, hidden):
@@ -329,20 +303,12 @@
     return call(
         unpack_kernel,
         [((128, 1024), BF), ((128, 1024), BF), ((1, 128), F32)],
-        [VMEM, VMEM, HBM, HBM],
-        [HBM, HBM, VMEM],
+        [VMEM] * 4,
+        [VMEM] * 3,
         400000000,
         2000000,
-        [
-            pltpu.VMEM((256, 2048), BF),
-            pltpu.VMEM((1, 128), F32),
-            pltpu.VMEM((128, 1024), BF),
-            pltpu.VMEM((128, 1024), BF),
-            pltpu.VMEM((128, 1024), BF),
-            pltpu.SemaphoreType.DMA((2,)),
-            pltpu.SemaphoreType.DMA((2,)),
-        ],
-    )(recv, place, hbm(gates), hbm(cot))
+        [pltpu.VMEM((256, 2048), BF)],
+    )(recv, place, gates, cot)
 
 
 def sum_grads(parts):
@@ -369,20 +335,20 @@
 
     ids = expert_ids.reshape(1, 128)
     gate_row = gates.reshape(1, 128)
-    own, send, place = pack(ids, gate_row, x_rows, cotangent, w_gate, w_up, w_down)
+    own, send, place, gate_kept = pack(ids, gate_row, x_rows, cotangent, w_gate, w_up, w_down)
     shards = []
     for k in (1, 2, 3):
         shards.append(shift(own, k))
     recv = exchange(send)
     index = lax.axis_index("dp").astype(jnp.int32).reshape(1)
-    out, g2, rows, slopes, hidden = expert_rows(index, recv, w_gate, w_up, w_down, shards)
+    out, g2, rows, slopes, hidden = expert_rows(index, recv, [own, *shards])
     returned = exchange(out)
     r2 = shift(g2, 2)
     g1, g3, g0 = other_grads(index, rows, slopes, hidden)
     r1 = shift(g1, 1)
     r3 = shift(g3, 3)
     parts = (g0, r1, r2, r3)
-    gated_out, input_grad, gate_grad = unpack_rows(returned, place, gate_row, cotangent)
+    gated_out, input_grad, gate_grad = unpack_rows(returned, place, gate_kept, cotangent)
     grads = sum_grads(parts)
     return (gated_out, input_grad, gate_grad.reshape(128, 1), *grads)
 

time: 112 us -> 110 us (0.982)
  Pallas kernels: 12.1 us -> 10.3 us
    pallas_call x1, Pallas kernels: 2.64 us -> 1.41 us  [unpack_rows(): call(unpack_kernel, [((128, 1024), BF), ((128, 1024), BF), ((1, 128), F32...]
  transfers between devices with their start and end apart: 8 -> 8, of which waited for: 5 -> 5; matrix products, arithmetic and copies ran while one was open for 0% -> 0% of each run, Pallas kernels for 1% -> 2%
where the time goes in v4:
time: 110 us
  starting transfers between devices  50.6 us (46%)
  waiting for transfers between devices  48.2 us (44%)
  Pallas kernels  10.3 us (9%)
    ppermute x6, waiting for transfers between devices, shift(): lax.ppermute(value, 'dp', [(i, (i + k) % groups) for i in range(groups)])  48.2 us
    all_to_all x2, starting transfers between devices, exchange(): lax.all_to_all(wire, 'expert', split_axis=0, concat_axis=0, tiled=True)  32.4 us
    ppermute x6, starting transfers between devices, shift(): lax.ppermute(value, 'dp', [(i, (i + k) % groups) for i in range(groups)])  18.2 us
    pallas_call x1, Pallas kernels, expert_rows(): call(expert_kernel, [((2048, 256), BF), ((1152, 256), BF, True), ((8, 256...  4.35 us
    pallas_call x1, Pallas kernels, pack(): call(pack_kernel, [((1152, 256), BF), ((2048, 256), BF), ((256, 128), BF)...  2.84 us
  transfers between devices with their start and end apart: 8, of which 5 were waited for; matrix products, arithmetic and copies ran while one was open for 0% of the time, Pallas kernels for 2%

profile of v4, /device:TPU:1, one launch (start us, length us, event | category | flops | bytes accessed | tf_op | source)
XLA Modules:
  0.0 109.9 jit_solution(17472299307347596668)
XLA Ops:
  0.6 2.8 %shard_map.118 = (bf16[1152,256]{1,0:T(8,128)(2,1)S(1)}, bf16[2048,256]{1,0:T(8,128)(2,1)}, bf16[256,128]{1,0:T(8,128)(2,1)S(1)}, f32[1,128]{1,0:T(1,128)S(1)}) custom-call(s32[1,128]{1,0:T(1,128)} %bitcast.10, f32[1,128]{1,0:T(1,128)} %bitcast.11, bf16[128,1024]{1,0:T(8,128)(2,1)} %x.1, bf16[128,1024]{1,0:T(8,128)(2,1)} %cot.3, bf16[1,256,384]{2,1,0:T(8,128)(2,1)} %wg.1, ...), custom_call_target="tpu_custom_call" | custom-call | flops 400000000 | bytes 2600000 | tf_op jit(solution)/shard_map/pallas_call | solution.py:251
  3.5 18.4 %all-to-all-start = ((bf16[128,16,256]{2,1,0:T(8,128)(2,1)}), bf16[128,16,256]{2,1,0:T(8,128)(2,1)S(1)}, u32[]{:S(2)}, u32[]{:S(2)}) async-start(bf16[128,16,256]{2,1,0:T(8,128)(2,1)} %bitcast.3), calls=%async_computation | async-start | bytes 2097152 | tf_op jit(solution)/shard_map/all_to_all | solution.py:333
  21.9 4.4 %collective-permute-start.2 = (bf16[1152,256]{1,0:T(8,128)(2,1)S(1)}, bf16[1152,256]{1,0:T(8,128)(2,1)S(1)}, u32[]{:S(2)}, u32[]{:S(2)}) collective-permute-start(bf16[1152,256]{1,0:T(8,128)(2,1)S(1)} %get-tuple-element.25.w0), channel_id=1, source_target_pairs={{0,384},{128,0},{256,128},{384,256},{1,385},{129,1},{257,129},{385... | collective-permute-start | bytes 1769480 | tf_op jit(solution)/shard_map/ppermute | solution.py:329
  26.3 2.4 %collective-permute-start.1 = (bf16[1152,256]{1,0:T(8,128)(2,1)S(1)}, bf16[1152,256]{1,0:T(8,128)(2,1)S(1)}, u32[]{:S(2)}, u32[]{:S(2)}) collective-permute-start(bf16[1152,256]{1,0:T(8,128)(2,1)S(1)} %get-tuple-element.25.w0), channel_id=1, source_target_pairs={{0,256},{128,384},{256,0},{384,128},{1,257},{129,385},{257,1},{385... | collective-permute-start | bytes 1769480 | tf_op jit(solution)/shard_map/ppermute | solution.py:329
  28.7 2.5 %collective-permute-start = (bf16[1152,256]{1,0:T(8,128)(2,1)S(1)}, bf16[1152,256]{1,0:T(8,128)(2,1)S(1)}, u32[]{:S(2)}, u32[]{:S(2)}) collective-permute-start(bf16[1152,256]{1,0:T(8,128)(2,1)S(1)} %get-tuple-element.25.w0), channel_id=1, source_target_pairs={{0,128},{128,256},{256,384},{384,0},{1,129},{129,257},{257,385},{3... | collective-permute-start | bytes 1769480 | tf_op jit(solution)/shard_map/ppermute | solution.py:329
  31.3 7.6 %collective-permute-done.2.w3 = bf16[1152,256]{1,0:T(8,128)(2,1)S(1)} collective-permute-done((bf16[1152,256]{1,0:T(8,128)(2,1)S(1)}, bf16[1152,256]{1,0:T(8,128)(2,1)S(1)}, u32[]{:S(2)}, u32[]{:S(2)}) %collective-permute-start.2) | collective-permute-done | bytes 589856 | tf_op jit(solution)/shard_map/ppermute | solution.py:329
  38.9 4.6 %collective-permute-done.1.w2 = bf16[1152,256]{1,0:T(8,128)(2,1)S(1)} collective-permute-done((bf16[1152,256]{1,0:T(8,128)(2,1)S(1)}, bf16[1152,256]{1,0:T(8,128)(2,1)S(1)}, u32[]{:S(2)}, u32[]{:S(2)}) %collective-permute-start.1) | collective-permute-done | bytes 589856 | tf_op jit(solution)/shard_map/ppermute | solution.py:329
  43.5 14.1 %collective-permute-done.w1 = bf16[1152,256]{1,0:T(8,128)(2,1)S(1)} collective-permute-done((bf16[1152,256]{1,0:T(8,128)(2,1)S(1)}, bf16[1152,256]{1,0:T(8,128)(2,1)S(1)}, u32[]{:S(2)}, u32[]{:S(2)}) %collective-permute-start) | collective-permute-done | bytes 589856 | tf_op jit(solution)/shard_map/ppermute | solution.py:329
  57.6 0.0 all-to-all-done
  57.6 4.3 %shard_map.119 = (bf16[2048,256]{1,0:T(8,128)(2,1)}, bf16[1152,256]{1,0:T(8,128)(2,1)}, bf16[8,256,256]{2,1,0:T(8,128)(2,1)}, bf16[3,256,256]{2,1,0:T(8,128)(2,1)}, bf16[256,384]{1,0:T(8,128)(2,1)}) custom-call(s32[1]{0:T(128)} %bitcast.index, bf16[2048,256]{1,0:T(8,128)(2,1)S(1)} %bitcast.9, bf16[1152,256]{1,0:T(8,128)(2,1)S(1)} %get-tuple-element.25.w0, ...), custom_call_target="tpu_custom_call" | custom-call | flops 2000000000 | bytes 6000000 | tf_op jit(solution)/shard_map/pallas_call | solution.py:270
  61.9 0.0 copy-start.1
  62.0 0.0 copy-start.2
  62.0 0.0 copy-start.3
  62.0 14.0 %all-to-all-start.1 = ((bf16[128,16,256]{2,1,0:T(8,128)(2,1)}), bf16[128,16,256]{2,1,0:T(8,128)(2,1)S(1)}, u32[]{:S(2)}, u32[]{:S(2)}) async-start(bf16[128,16,256]{2,1,0:T(8,128)(2,1)} %bitcast.5), calls=%async_computation.1 | async-start | bytes 2097152 | tf_op jit(solution)/shard_map/all_to_all | solution.py:333
  76.0 2.4 %collective-permute-start.4 = (bf16[1152,256]{1,0:T(8,128)(2,1)}, bf16[1152,256]{1,0:T(8,128)(2,1)S(1)}, u32[]{:S(2)}, u32[]{:S(2)}) collective-permute-start(bf16[1152,256]{1,0:T(8,128)(2,1)} %get-tuple-element.37), channel_id=1, source_target_pairs={{0,256},{128,384},{256,0},{384,128},{1,257},{129,385},{257,1},{385... | collective-permute-start | bytes 1769480 | tf_op jit(solution)/shard_map/ppermute | solution.py:329
  78.4 0.0 copy-done.1
  78.4 0.0 copy-done.2
  78.4 0.0 copy-done.3
  78.4 0.7 shard_map.121
  79.1 2.3 %collective-permute-start.3 = (bf16[1152,256]{1,0:T(8,128)(2,1)S(1)}, bf16[1152,256]{1,0:T(8,128)(2,1)S(1)}, u32[]{:S(2)}, u32[]{:S(2)}) collective-permute-start(bf16[1152,256]{1,0:T(8,128)(2,1)S(1)} %get-tuple-element.36), channel_id=1, source_target_pairs={{0,128},{128,256},{256,384},{384,0},{1,129},{129,257},{257,385},{3... | collective-permute-start | bytes 1769480 | tf_op jit(solution)/shard_map/ppermute | solution.py:329
  81.4 4.2 %collective-permute-start.5 = (bf16[1152,256]{1,0:T(8,128)(2,1)S(1)}, bf16[1152,256]{1,0:T(8,128)(2,1)S(1)}, u32[]{:S(2)}, u32[]{:S(2)}) collective-permute-start(bf16[1152,256]{1,0:T(8,128)(2,1)S(1)} %get-tuple-element.38), channel_id=1, source_target_pairs={{0,384},{128,0},{256,128},{384,256},{1,385},{129,1},{257,129},{385... | collective-permute-start | bytes 1769480 | tf_op jit(solution)/shard_map/ppermute | solution.py:329
  85.6 8.0 %collective-permute-done.4.r2 = bf16[1152,256]{1,0:T(8,128)(2,1)S(1)} collective-permute-done((bf16[1152,256]{1,0:T(8,128)(2,1)}, bf16[1152,256]{1,0:T(8,128)(2,1)S(1)}, u32[]{:S(2)}, u32[]{:S(2)}) %collective-permute-start.4) | collective-permute-done | bytes 589856 | tf_op jit(solution)/shard_map/ppermute | solution.py:329
  93.6 13.9 %collective-permute-done.3.r1 = bf16[1152,256]{1,0:T(8,128)(2,1)S(1)} collective-permute-done((bf16[1152,256]{1,0:T(8,128)(2,1)S(1)}, bf16[1152,256]{1,0:T(8,128)(2,1)S(1)}, u32[]{:S(2)}, u32[]{:S(2)}) %collective-permute-start.3) | collective-permute-done | bytes 589856 | tf_op jit(solution)/shard_map/ppermute | solution.py:329
  107.5 0.0 collective-permute-done.5.r3
  107.5 0.0 copy-start
  107.5 1.0 shard_map.122
  108.4 0.0 all-to-all-done.1
  108.4 0.0 copy-done
  108.4 1.4 %shard_map.120 = (bf16[128,1024]{1,0:T(8,128)(2,1)}, bf16[128,1024]{1,0:T(8,128)(2,1)}, f32[1,128]{1,0:T(1,128)}) custom-call(bf16[2048,256]{1,0:T(8,128)(2,1)S(1)} %bitcast.8, bf16[256,128]{1,0:T(8,128)(2,1)S(1)} %get-tuple-element.27.place, f32[1,128]{1,0:T(1,128)S(1)} %get-tuple-element.28.gates, bf16[128,1024]{1,0:T(8,128)(2,1)S(1)} %copy-done), custom_call_target="tpu_custom_call" | custom-call | flops 400000000 | bytes 2000000 | tf_op jit(solution)/shard_map/pallas_call | solution.py:303
Async XLA Ops:
  3.5 54.1 %all-to-all-start = ((bf16[128,16,256]{2,1,0:T(8,128)(2,1)}), bf16[128,16,256]{2,1,0:T(8,128)(2,1)S(1)}, u32[]{:S(2)}, u32[]{:S(2)}) async-start(bf16[128,16,256]{2,1,0:T(8,128)(2,1)} %bitcast.3), calls=%async_computation | async-start | bytes 2097152 | tf_op jit(solution)/shard_map/all_to_all | solution.py:333
  21.9 17.0 %collective-permute-start.2 = (bf16[1152,256]{1,0:T(8,128)(2,1)S(1)}, bf16[1152,256]{1,0:T(8,128)(2,1)S(1)}, u32[]{:S(2)}, u32[]{:S(2)}) collective-permute-start(bf16[1152,256]{1,0:T(8,128)(2,1)S(1)} %get-tuple-element.25.w0), channel_id=1, source_target_pairs={{0,384},{128,0},{256,128},{384,256},{1,385},{129,1},{257,129},{385... | collective-permute-start | bytes 1769480 | tf_op jit(solution)/shard_map/ppermute | solution.py:329
  26.3 17.2 %collective-permute-start.1 = (bf16[1152,256]{1,0:T(8,128)(2,1)S(1)}, bf16[1152,256]{1,0:T(8,128)(2,1)S(1)}, u32[]{:S(2)}, u32[]{:S(2)}) collective-permute-start(bf16[1152,256]{1,0:T(8,128)(2,1)S(1)} %get-tuple-element.25.w0), channel_id=1, source_target_pairs={{0,256},{128,384},{256,0},{384,128},{1,257},{129,385},{257,1},{385... | collective-permute-start | bytes 1769480 | tf_op jit(solution)/shard_map/ppermute | solution.py:329
  28.7 28.8 %collective-permute-start = (bf16[1152,256]{1,0:T(8,128)(2,1)S(1)}, bf16[1152,256]{1,0:T(8,128)(2,1)S(1)}, u32[]{:S(2)}, u32[]{:S(2)}) collective-permute-start(bf16[1152,256]{1,0:T(8,128)(2,1)S(1)} %get-tuple-element.25.w0), channel_id=1, source_target_pairs={{0,128},{128,256},{256,384},{384,0},{1,129},{129,257},{257,385},{3... | collective-permute-start | bytes 1769480 | tf_op jit(solution)/shard_map/ppermute | solution.py:329
  61.9 16.5 %copy-start.1 = (bf16[8,256,256]{2,1,0:T(8,128)(2,1)S(1)}, bf16[8,256,256]{2,1,0:T(8,128)(2,1)}, u32[]{:S(2)}) copy-start(bf16[8,256,256]{2,1,0:T(8,128)(2,1)} %get-tuple-element.32.rows) | copy-start | bytes 3145732
  62.0 16.5 %copy-start.2 = (bf16[3,256,256]{2,1,0:T(8,128)(2,1)S(1)}, bf16[3,256,256]{2,1,0:T(8,128)(2,1)}, u32[]{:S(2)}) copy-start(bf16[3,256,256]{2,1,0:T(8,128)(2,1)} %get-tuple-element.33.slopes) | copy-start | bytes 1179652
  62.0 16.5 %copy-start.3 = (bf16[256,384]{1,0:T(8,128)(2,1)S(1)}, bf16[256,384]{1,0:T(8,128)(2,1)}, u32[]{:S(2)}) copy-start(bf16[256,384]{1,0:T(8,128)(2,1)} %get-tuple-element.34.hidden) | copy-start | bytes 589828
  62.0 46.5 %all-to-all-start.1 = ((bf16[128,16,256]{2,1,0:T(8,128)(2,1)}), bf16[128,16,256]{2,1,0:T(8,128)(2,1)S(1)}, u32[]{:S(2)}, u32[]{:S(2)}) async-start(bf16[128,16,256]{2,1,0:T(8,128)(2,1)} %bitcast.5), calls=%async_computation.1 | async-start | bytes 2097152 | tf_op jit(solution)/shard_map/all_to_all | solution.py:333
  76.0 17.6 %collective-permute-start.4 = (bf16[1152,256]{1,0:T(8,128)(2,1)}, bf16[1152,256]{1,0:T(8,128)(2,1)S(1)}, u32[]{:S(2)}, u32[]{:S(2)}) collective-permute-start(bf16[1152,256]{1,0:T(8,128)(2,1)} %get-tuple-element.37), channel_id=1, source_target_pairs={{0,256},{128,384},{256,0},{384,128},{1,257},{129,385},{257,1},{385... | collective-permute-start | bytes 1769480 | tf_op jit(solution)/shard_map/ppermute | solution.py:329
  79.1 28.3 %collective-permute-start.3 = (bf16[1152,256]{1,0:T(8,128)(2,1)S(1)}, bf16[1152,256]{1,0:T(8,128)(2,1)S(1)}, u32[]{:S(2)}, u32[]{:S(2)}) collective-permute-start(bf16[1152,256]{1,0:T(8,128)(2,1)S(1)} %get-tuple-element.36), channel_id=1, source_target_pairs={{0,128},{128,256},{256,384},{384,0},{1,129},{129,257},{257,385},{3... | collective-permute-start | bytes 1769480 | tf_op jit(solution)/shard_map/ppermute | solution.py:329
  81.4 26.0 %collective-permute-start.5 = (bf16[1152,256]{1,0:T(8,128)(2,1)S(1)}, bf16[1152,256]{1,0:T(8,128)(2,1)S(1)}, u32[]{:S(2)}, u32[]{:S(2)}) collective-permute-start(bf16[1152,256]{1,0:T(8,128)(2,1)S(1)} %get-tuple-element.38), channel_id=1, source_target_pairs={{0,384},{128,0},{256,128},{384,256},{1,385},{129,1},{257,129},{385... | collective-permute-start | bytes 1769480 | tf_op jit(solution)/shard_map/ppermute | solution.py:329
  107.5 1.0 copy-start
